TPU v7x, 512 devices: a whole 4x8x8 slice. The times are simulated.
512 devices in a mesh: row: 128 (over z, y, core), ex: 4 (over x).
Axes of the slice: x: 4, y: 8, z: 8, core: 2. Of those that a mesh axis runs over, the one named last changes fastest.
Arguments:
- grads: bfloat16 [1, 4, 2048, 2048], P(None, 'ex', 'row'), may hold values from -6 to 6
- right_inv: bfloat16 [2048, 2048], P('row', 'ex'), may hold values from -0.125 to 0.125
- left_inv: bfloat16 [2048, 2048], P(('row', 'ex')), may hold values from -0.125 to 0.125
- row_signs: int32 [1, 4, 2048], replicated, may hold values from 0 to 1
- col_signs: int32 [1, 4, 2048], replicated, may hold values from 0 to 1
- listed: int32 [1, 128, 4, 32], P(None, 'row', 'ex'), may hold values from 0 to 32767, as said below
- owners: int32 [1, 128, 4, 32, 1], P(None, 'row'), may hold values from 0 to 127; in each aligned block of 128 rows (0 to 127, 128 to 255, ..., all dimensions but the last counted through in order) at most 2 rows name the same one
Outputs:
- sketch: float32 [1, 128, 128, 2, 256], P(None, 'row')
Inputs may be any that keep to these rules, and one draw needn't show every extreme that they name: `listed`: for each batch b, group g and example x, the 32 entries name distinct blocks in ascending order, all from g * 256 to (g + 1) * 256 - 1. `owners`: within one batch and group, no owner is named by more than 2 of the 128 entries, a bound that some block reaches.
All inputs are finite; a program needn't handle non-finite values.
Results may differ from a plain program's by a relative error of at most 0.0029.
Values may be sent and summed in bfloat16 or wider, within the bound.
No kernel may reach another device: no remote copies, remote signals or barrier semaphores. Data moves between devices by JAX's collectives and lax.ppermute only.
A program may use at most 64 MiB of HBM per device.

v0:
```python
import math

import jax
import jax.numpy as jnp
import numpy as np
from jax import lax
from jax.experimental import pallas as pl
from jax.experimental.pallas import tpu as pltpu
from jax.sharding import Mesh
from jax.sharding import PartitionSpec as P


DM = 2048
BLOCK = 128
NZ, NY, NC, NE = 8, 8, 2, 4
NYC = NY * NC
ROWS = NZ * NYC
GROUP_ROWS = DM // ROWS
TILE_ROWS = DM // NZ
RADIX = 8
INNER = DM // RADIX
ROOT_HALF = math.sqrt(0.5)

f32 = jnp.float32
bf16 = jnp.bfloat16
ROW_AXES = ("z", "y", "c")
IN_VMEM = pl.BlockSpec(memory_space=pltpu.VMEM)
IN_SMEM = pl.BlockSpec(memory_space=pltpu.SMEM)


def split_table(table):
    high = table.astype(bf16)
    low = (table - high.astype(np.float64)).astype(bf16)
    return high, low


def dft_angles(rows, cols, length):
    return 2.0 * math.pi * ((np.arange(rows)[:, None] * np.arange(cols)[None, :]) % length) / length


def column_tables():
    angles = dft_angles(INNER, INNER, INNER)
    high, low = split_table(np.concatenate([np.cos(angles), -np.sin(angles)], axis=0))
    angles = dft_angles(INNER, RADIX, DM)
    twiddles = np.concatenate([np.cos(angles), -np.sin(angles)], axis=1).astype(np.float32)
    return high, low, twiddles


def row_tables():
    angles = dft_angles(BLOCK, BLOCK, BLOCK)
    real, imag = np.cos(angles), -np.sin(angles)
    full = np.concatenate(
        [np.concatenate([real, imag], axis=1), np.concatenate([-imag, real], axis=1)], axis=0
    )
    high, low = split_table(full)
    angles = dft_angles(NYC, BLOCK, DM)
    twiddles = np.stack([np.cos(angles), -np.sin(angles)]).astype(np.float32)
    return high, low, twiddles.reshape(2, NYC, 1, BLOCK)


def add(a, b):
    return (a[0] + b[0], a[1] + b[1])


def sub(a, b):
    return (a[0] - b[0], a[1] - b[1])


def mul(a, b):
    return (a[0] * b[0] - a[1] * b[1], a[0] * b[1] + a[1] * b[0])


def minus_i(a):
    return (a[1], -a[0])


def fft4(a, b, c, d):
    even, odd = add(a, c), sub(a, c)
    even2, odd2 = add(b, d), minus_i(sub(b, d))
    return [add(even, even2), add(odd, odd2), sub(even, even2), sub(odd, odd2)]


def fft8(terms):
    even = fft4(terms[0], terms[2], terms[4], terms[6])
    odd = fft4(terms[1], terms[3], terms[5], terms[7])
    one = ((odd[1][0] + odd[1][1]) * ROOT_HALF, (odd[1][1] - odd[1][0]) * ROOT_HALF)
    three = ((odd[3][1] - odd[3][0]) * ROOT_HALF, (odd[3][0] + odd[3][1]) * -ROOT_HALF)
    turned = [odd[0], one, minus_i(odd[2]), three]
    return [add(e, o) for e, o in zip(even, turned)] + [sub(e, o) for e, o in zip(even, turned)]


def fft16(terms):
    inner = [fft4(*[terms[4 * a + b] for a in range(4)]) for b in range(4)]
    out = [None] * 16
    for first in range(4):
        column = []
        for b in range(4):
            turn = -2.0 * math.pi * b * first / 16
            value = inner[b][first]
            if b * first:
                cos, sin = math.cos(turn), math.sin(turn)
                value = (value[0] * cos - value[1] * sin, value[0] * sin + value[1] * cos)
            column.append(value)
        for second, value in enumerate(fft4(*column)):
            out[first + 4 * second] = value
    return out


def dot(a, b):
    return jnp.dot(a, b, preferred_element_type=f32)


def deal_kernel(right, left, out):
    quarter = GROUP_ROWS // NE
    width = right.shape[1]
    pack = BLOCK // NE
    column = lax.broadcasted_iota(jnp.int32, (width, width), 0)
    target = lax.broadcasted_iota(jnp.int32, (width, width), 1)
    order = target == pack * (column % NYC) + column // NYC
    sorted_cols = dot(right[...], jnp.where(order, 1.0, 0.0).astype(bf16))
    tail = left[...].astype(f32)
    tail = jnp.concatenate([tail, tail], axis=0)
    shape = (2 * quarter, BLOCK)
    upper = lax.broadcasted_iota(jnp.int32, shape, 0) < quarter
    lane_group = lax.broadcasted_iota(jnp.int32, shape, 1) // pack
    for tile in range(width // BLOCK):
        lanes = slice(tile * BLOCK, (tile + 1) * BLOCK)
        row_groups = []
        for half in range(2):
            value = sorted_cols[2 * quarter * half : 2 * quarter * (half + 1), lanes]
            row_groups += [value, pltpu.roll(value, quarter, axis=0)]
        for group in range(NE):
            yc = tile * NE + group
            piece = None
            for p in range(NE):
                moved = row_groups[p]
                if p != group:
                    moved = pltpu.roll(moved, (pack * (p - group)) % BLOCK, axis=1)
                piece = moved if piece is None else jnp.where(lane_group == p, moved, piece)
            for z in range(NZ):
                zc = z * NC + yc % NC
                both = jnp.where(upper, piece, tail[:, zc * BLOCK : (zc + 1) * BLOCK])
                out[z * NYC + yc] = both.astype(bf16)


def arrange_kernel(pieces, right, left):
    quarter = GROUP_ROWS // NE
    pack = BLOCK // NE
    shape = (ROWS, 2 * quarter, BLOCK)
    first = lax.broadcasted_iota(jnp.int32, shape, 1) < quarter
    lane_group = lax.broadcasted_iota(jnp.int32, shape, 2) // pack
    values = [pieces[e].astype(f32) for e in range(NE)]
    unpacked = []
    for p in range(NE):
        rows = None
        for e in range(NE):
            moved = values[e]
            if e != p:
                moved = pltpu.roll(moved, (pack * (e - p)) % BLOCK, axis=2)
            rows = moved if rows is None else jnp.where(lane_group == e, moved, rows)
        unpacked.append(rows)
    rights, lefts = [], []
    for e in range(0, NE, 2):
        rights.append(jnp.where(first, unpacked[e], pltpu.roll(unpacked[e + 1], quarter, axis=1)))
        lefts.append(jnp.where(first, pltpu.roll(values[e], quarter, axis=1), values[e + 1]))
    right[...] = jnp.concatenate(rights, axis=1).astype(bf16)
    left[...] = jnp.concatenate(lefts, axis=1).astype(bf16)


def project_kernel(place, own, other, right, col_flip, out):
    factor = right[...].reshape(DM, BLOCK)
    for side, rows in enumerate((own, other)):
        part = dot(rows[...].reshape(TILE_ROWS // NC, DM), factor) * col_flip[...]
        part = part.astype(bf16).reshape(NY, GROUP_ROWS, BLOCK)
        for k in range(NY):
            from_y = (place[0] + NY // 2 + k) % NY
            from_c = place[1] if side == 0 else 1 - place[1]
            start = pl.multiple_of(GROUP_ROWS * (NC * from_y + from_c), GROUP_ROWS)
            out[pl.ds(start, GROUP_ROWS), :] = part[k]


def whiten_kernel(place, tile, own, other, row_flip, high, low, twiddles, out, white, stage):
    left = jnp.concatenate([own[...].reshape(DM, BLOCK), other[...].reshape(DM, BLOCK)], axis=1)
    half = TILE_ROWS // NC
    starts = [pl.multiple_of(half * side, half) for side in (place[1], 1 - place[1])]
    halves = [tile[pl.ds(start, half), :] for start in starts]
    white[...] = dot(left, jnp.concatenate(halves, axis=0)) * row_flip[...]
    for p in range(0, RADIX, 2):
        pair = [white[pl.ds(p + k, INNER, stride=RADIX), :] for k in range(2)]
        part = jnp.concatenate(pair, axis=1)
        part_high = part.astype(bf16)
        part_low = (part - part_high.astype(f32)).astype(bf16)
        both = dot(high[...], part_high) + dot(low[...], part_high) + dot(high[...], part_low)
        stage[p] = both[:, 0:BLOCK]
        stage[p + 1] = both[:, BLOCK:]

    def combine(step, carry):
        rows = pl.ds(pl.multiple_of(step * GROUP_ROWS, GROUP_ROWS), GROUP_ROWS)
        rows_imag = pl.ds(pl.multiple_of(INNER + step * GROUP_ROWS, GROUP_ROWS), GROUP_ROWS)
        factors = twiddles[rows, :]
        terms = [(stage[0, rows, :], stage[0, rows_imag, :])]
        for p in range(1, RADIX):
            factor = (factors[:, p : p + 1], factors[:, RADIX + p : RADIX + p + 1])
            terms.append(mul((stage[p, rows, :], stage[p, rows_imag, :]), factor))
        for k, value in enumerate(fft8(terms)):
            out[NYC * k + step, 0:GROUP_ROWS, :] = value[0].astype(bf16)
            out[NYC * k + step, GROUP_ROWS : 2 * GROUP_ROWS, :] = value[1].astype(bf16)
        return carry

    lax.fori_loop(0, INNER // GROUP_ROWS, combine, 0, unroll=4)


def spectrum_kernel(parts, cross, turns, high, low, wanted, out, mixed):
    for yc in range(NYC):
        total = parts[yc].astype(f32)
        for z in range(1, NZ):
            total = total + parts[z * NYC + yc].astype(f32)
        value = mul((total[0:GROUP_ROWS], total[GROUP_ROWS:]), (cross[0, yc], cross[1, yc]))
        mixed[yc, :, 0:BLOCK] = value[0]
        mixed[yc, :, BLOCK : 2 * BLOCK] = value[1]
    rows = mixed[...].reshape(NYC * GROUP_ROWS, 2 * BLOCK)
    rows_high = rows.astype(bf16)
    rows_low = (rows - rows_high.astype(f32)).astype(bf16)
    rows = dot(rows_high, high[...]) + dot(rows_low, high[...]) + dot(rows_high, low[...])
    rows = rows.reshape(NYC, GROUP_ROWS, 2 * BLOCK)
    terms = [
        mul((rows[yc, :, 0:BLOCK], rows[yc, :, BLOCK:]), (turns[0, yc], turns[1, yc]))
        for yc in range(NYC)
    ]
    blocks = [jnp.concatenate(value, axis=1).astype(bf16) for value in fft16(terms)]
    blocks = jnp.concatenate(blocks, axis=0)
    row = lax.broadcasted_iota(jnp.int32, (out.shape[0], NYC * GROUP_ROWS), 1)
    chosen = jnp.where(row == wanted[...], 1.0, 0.0).astype(bf16)
    out[...] = dot(chosen, blocks).astype(bf16)


def grant(mebibytes):
    return pltpu.CompilerParams(vmem_limit_bytes=mebibytes * 2**20)


def near(array):
    return pltpu.with_memory_space_constraint(array, pltpu.VMEM)


def shift_y(rows, step):
    return lax.ppermute(rows, "y", [(i, (i + step) % NY) for i in range(NY)])


def shards(grads, right_inv, left_inv, row_signs, col_signs, listed, owners):
    z_id, y_id, c_id, e_id = (lax.axis_index(name) for name in ("z", "y", "c", "e"))
    yc_id = y_id * NC + c_id
    row_id = z_id * NYC + yc_id
    list_len = listed.shape[3]
    capacity = 2

    pieces = pl.pallas_call(
        deal_kernel,
        out_shape=pltpu.VMEM((ROWS, 2 * GROUP_ROWS // NE, BLOCK), bf16),
        in_specs=[IN_VMEM] * 2,
        out_specs=IN_VMEM,
        compiler_params=grant(8),
        name="deal",
    )(right_inv, left_inv)
    pieces = lax.all_to_all(pieces, ROW_AXES, 0, 0, tiled=True)
    pieces = lax.all_to_all(jnp.broadcast_to(pieces[None], (NE,) + pieces.shape), "e", 0, 0, tiled=True)

    swap = [(0, 1), (1, 0)]
    mine = grads.reshape(1, GROUP_ROWS, DM)
    near_rows = jnp.concatenate([shift_y(mine, 1), mine, shift_y(mine, -1)])
    rows_own = jnp.concatenate([shift_y(near_rows, 3), near_rows, shift_y(near_rows[:2], -3)])
    rows_other = lax.ppermute(rows_own, "c", swap)
    factor_shape = pltpu.VMEM((ROWS, GROUP_ROWS, BLOCK), bf16)
    right_cols, left_own = pl.pallas_call(
        arrange_kernel,
        out_shape=(factor_shape, factor_shape),
        in_specs=[IN_VMEM],
        out_specs=(IN_VMEM, IN_VMEM),
        compiler_params=grant(12),
        name="arrange",
    )(near(pieces))
    left_other = lax.ppermute(left_own, "c", swap)
    place = jnp.stack([y_id, c_id])

    row_bits = lax.dynamic_index_in_dim(row_signs[0], e_id, 0, keepdims=False)
    row_flip = (1 - 2 * row_bits).astype(f32)[:, None]
    col_bits = lax.dynamic_index_in_dim(col_signs[0], e_id, 0, keepdims=False)
    col_bits = col_bits.reshape(BLOCK, NYC)
    own_col = jnp.arange(NYC, dtype=jnp.int32) == yc_id
    col_bits = jnp.sum(jnp.where(own_col[None, :], col_bits, 0), axis=1)[None, :]
    col_flip = (1 - 2 * col_bits).astype(f32)
    high, low, twiddles = column_tables()
    tile = pl.pallas_call(
        project_kernel,
        out_shape=pltpu.VMEM((TILE_ROWS, BLOCK), bf16),
        in_specs=[IN_SMEM] + [IN_VMEM] * 4,
        out_specs=IN_VMEM,
        compiler_params=grant(6),
        name="project",
    )(place, near(rows_own), near(rows_other), near(right_cols), col_flip)
    partial_cols = pl.pallas_call(
        whiten_kernel,
        out_shape=pltpu.VMEM((ROWS, 2 * GROUP_ROWS, BLOCK), bf16),
        in_specs=[IN_SMEM] + [IN_VMEM] * 7,
        out_specs=IN_VMEM,
        scratch_shapes=[
            pltpu.VMEM((DM, BLOCK), f32),
            pltpu.VMEM((RADIX, 2 * INNER, BLOCK), f32),
        ],
        compiler_params=grant(16),
        name="whiten",
    )(place, near(tile), near(left_own), near(left_other), row_flip, high, low, twiddles)
    partial_rows = lax.all_to_all(partial_cols, ROW_AXES, 0, 0, tiled=True)

    spectrum_rows = row_id * GROUP_ROWS + jnp.arange(GROUP_ROWS, dtype=jnp.int32)
    columns = jnp.arange(NYC, dtype=jnp.int32)[:, None] + NYC * jnp.arange(BLOCK, dtype=jnp.int32)
    columns = columns.reshape(NYC, 1, BLOCK)
    phase = spectrum_rows[None, :, None] * columns
    angle = phase.astype(f32) * (2.0 * math.pi / (DM * DM))
    cross = jnp.stack([jnp.cos(angle), -jnp.sin(angle)]) * (1.0 / DM)
    local_ids = listed[0, 0, 0] - row_id * (GROUP_ROWS * NYC)
    wanted = (local_ids % NYC) * GROUP_ROWS + local_ids // NYC
    row_high, row_low, turns = row_tables()
    picked = pl.pallas_call(
        spectrum_kernel,
        out_shape=pltpu.VMEM((list_len, 2 * BLOCK), bf16),
        in_specs=[IN_VMEM] * 6,
        out_specs=IN_VMEM,
        scratch_shapes=[pltpu.VMEM((NYC, GROUP_ROWS, 2 * BLOCK), f32)],
        compiler_params=grant(12),
        name="spectrum",
    )(near(partial_rows), near(cross), turns, row_high, row_low, wanted[:, None])

    entries = lax.all_to_all(
        jnp.broadcast_to(picked[None], (NE,) + picked.shape), "e", 0, 0, tiled=True
    ).reshape(NE * list_len, 2 * BLOCK)
    owner_ids = owners[0, 0, :, :, 0].reshape(-1)
    order = jnp.arange(NE * list_len, dtype=jnp.int32)
    same = (owner_ids[:, None] == owner_ids[None, :]) & (order[:, None] < order[None, :])
    position = owner_ids * capacity + jnp.sum(same.astype(jnp.int32), axis=0)
    place = jnp.arange(ROWS * capacity, dtype=jnp.int32)[:, None] == position[None, :]
    outgoing = dot(place.astype(bf16), entries).astype(bf16)
    outgoing = outgoing.reshape(ROWS, capacity, 2 * BLOCK)
    arrived = lax.all_to_all(outgoing, ROW_AXES, 0, 0, tiled=True)
    return arrived.astype(f32)[None, None]


def solution(mesh):
    split = Mesh(mesh.devices.reshape(NZ, NY, NC, NE), ("z", "y", "c", "e"))
    in_specs = (
        P(None, "e", ROW_AXES, None),
        P(ROW_AXES, "e"),
        P(ROW_AXES + ("e",), None),
        P(),
        P(),
        P(None, ROW_AXES, "e", None),
        P(None, ROW_AXES, None, None, None),
    )
    out_specs = P(None, ROW_AXES, None, None, None)
    return jax.shard_map(shards, mesh=split, in_specs=in_specs, out_specs=out_specs, check_vma=False)
```

profile of v0, /device:TPU:1, one launch (start us, length us, event | category | flops | bytes accessed | tf_op | source)
XLA Modules:
  0.0 154.0 jit_solution(2121408312941885918)
XLA Ops:
  0.0 0.0 copy-start
  0.0 4.1 %collective-permute-start = (bf16[1,16,2048]{2,1,0:T(8,128)(2,1)}, bf16[1,16,2048]{2,1,0:T(8,128)(2,1)S(1)}, u32[]{:S(2)}, u32[]{:S(2)}) collective-permute-start(bf16[1,16,2048]{2,1,0:T(8,128)(2,1)} %bitcast.16), channel_id=1, source_target_pairs={{0,8},{8,16},{16,24},{24,32},{32,40},{40,48},{48,56},{56,0},{1,9},... | collective-permute-start | bytes 196616 | tf_op jit(solution)/shard_map/ppermute | solution.py:246
  4.2 3.8 %collective-permute-start.1 = (bf16[1,16,2048]{2,1,0:T(8,128)(2,1)}, bf16[1,16,2048]{2,1,0:T(8,128)(2,1)S(1)}, u32[]{:S(2)}, u32[]{:S(2)}) collective-permute-start(bf16[1,16,2048]{2,1,0:T(8,128)(2,1)} %bitcast.17), channel_id=1, source_target_pairs={{0,56},{8,0},{16,8},{24,16},{32,24},{40,32},{48,40},{56,48},{1,57}... | collective-permute-start | bytes 196616 | tf_op jit(solution)/shard_map/ppermute | solution.py:246
  8.0 0.0 copy-start.7
  8.0 0.7 copy-done.7
  8.7 0.7 copy-done.8
  9.4 1.0 deal.1
  10.4 17.6 %all-to-all-start = ((bf16[128,8,128]{2,1,0:T(8,128)(2,1)}), bf16[128,8,128]{2,1,0:T(8,128)(2,1)S(1)}, u32[]{:S(2)}, u32[]{:S(2)}) async-start(bf16[128,8,128]{2,1,0:T(8,128)(2,1)} %deal.1), calls=%async_computation | async-start | bytes 524288 | tf_op jit(solution)/shard_map/all_to_all | solution.py:264
  28.1 0.8 convert_bitcast_fusion
  28.9 0.0 copy-done
  28.9 0.1 reshape.206
  29.0 0.0 copy-start.9
  29.0 0.4 copy.23.row_flip
  29.4 0.0 collective-permute-done
  29.4 0.0 collective-permute-done.1
  29.4 0.4 copy-done.9
  29.9 5.1 %collective-permute-start.2 = (bf16[3,16,2048]{2,1,0:T(8,128)(2,1)S(1)}, bf16[3,16,2048]{2,1,0:T(8,128)(2,1)S(1)}, u32[]{:S(2)}, u32[]{:S(2)}) collective-permute-start(bf16[3,16,2048]{2,1,0:T(8,128)(2,1)S(1)} %pad_maximum_fusion), channel_id=1, source_target_pairs={{0,24},{8,32},{16,40},{24,48},{32,56},{40,0},{48,8},{56,16},{1,25}... | collective-permute-start | bytes 589832 | tf_op jit(solution)/shard_map/ppermute | solution.py:246
  35.0 3.2 %collective-permute-start.3 = (bf16[2,16,2048]{2,1,0:T(8,128)(2,1)S(1)}, bf16[2,16,2048]{2,1,0:T(8,128)(2,1)S(1)}, u32[]{:S(2)}, u32[]{:S(2)}) collective-permute-start(bf16[2,16,2048]{2,1,0:T(8,128)(2,1)S(1)} %pad_maximum_fusion.1), channel_id=1, source_target_pairs={{0,40},{8,48},{16,56},{24,0},{32,8},{40,16},{48,24},{56,32},{1,41}... | collective-permute-start | bytes 393224 | tf_op jit(solution)/shard_map/ppermute | solution.py:246
  38.2 12.6 %collective-permute-done.2 = bf16[3,16,2048]{2,1,0:T(8,128)(2,1)S(1)} collective-permute-done((bf16[3,16,2048]{2,1,0:T(8,128)(2,1)S(1)}, bf16[3,16,2048]{2,1,0:T(8,128)(2,1)S(1)}, u32[]{:S(2)}, u32[]{:S(2)}) %collective-permute-start.2) | collective-permute-done | bytes 196640 | tf_op jit(solution)/shard_map/ppermute | solution.py:246
  50.8 0.0 all-to-all-done
  50.8 1.1 broadcast_in_dim.21
  51.9 4.0 %all-to-all-start.1 = ((bf16[4,128,8,128]{3,2,1,0:T(8,128)(2,1)}), bf16[4,128,8,128]{3,2,1,0:T(8,128)(2,1)S(1)}, u32[]{:S(2)}, u32[]{:S(2)}) async-start(bf16[4,128,8,128]{3,2,1,0:T(8,128)(2,1)} %broadcast_in_dim.21), calls=%async_computation.1 | async-start | bytes 2097152 | tf_op jit(solution)/shard_map/all_to_all | solution.py:265
  56.0 0.0 collective-permute-done.3
  56.0 3.1 %collective-permute-start.4 = (bf16[8,16,2048]{2,1,0:T(8,128)(2,1)S(1)}, bf16[8,16,2048]{2,1,0:T(8,128)(2,1)S(1)}, u32[]{:S(2)}, u32[]{:S(2)}) collective-permute-start(bf16[8,16,2048]{2,1,0:T(8,128)(2,1)S(1)} %constant_dynamic-update-slice_fusion.own), channel_id=1, source_target_pairs={{0,4},{4,0},{1,5},{5,1},{2,6},{6,2},{3,7},{7,3},{8,12},{12,8},{9,1... | collective-permute-start | bytes 1572872 | tf_op jit(solution)/shard_map/ppermute | solution.py:271
  59.1 10.8 %all-to-all-done.1.pieces = bf16[4,128,8,128]{3,2,1,0:T(8,128)(2,1)S(1)} async-done(((bf16[4,128,8,128]{3,2,1,0:T(8,128)(2,1)}), bf16[4,128,8,128]{3,2,1,0:T(8,128)(2,1)S(1)}, u32[]{:S(2)}, u32[]{:S(2)}) %all-to-all-start.1) | async-done | bytes 1048608 | tf_op jit(solution)/shard_map/all_to_all | solution.py:265
  69.9 1.1 arrange.1
  71.0 4.0 %collective-permute-start.5 = (bf16[128,16,128]{2,1,0:T(8,128)(2,1)S(1)}, bf16[128,16,128]{2,1,0:T(8,128)(2,1)S(1)}, u32[]{:S(2)}, u32[]{:S(2)}) collective-permute-start(bf16[128,16,128]{2,1,0:T(8,128)(2,1)S(1)} %get-tuple-element.8.own), channel_id=1, source_target_pairs={{0,4},{4,0},{1,5},{5,1},{2,6},{6,2},{3,7},{7,3},{8,12},{12,8},{9,1... | collective-permute-start | bytes 1572872 | tf_op jit(solution)/shard_map/ppermute | solution.py:281
  75.0 0.1 pad_add_fusion.place
  75.1 0.1 select_reduce_fusion
  75.2 0.0 collective-permute-done.4.other
  75.3 0.0 copy-start.1
  75.3 0.0 copy-start.2
  75.3 0.0 copy-start.5
  75.3 1.0 project.1.tile
  76.3 0.3 collective-permute-done.5.other
  76.5 0.0 copy-done.1
  76.6 0.0 copy-done.2
  76.6 0.0 copy-done.5
  76.6 4.6 %whiten.1 = bf16[128,32,128]{2,1,0:T(8,128)(2,1)} custom-call(s32[2]{0:T(128)S(1)} %pad_add_fusion.place, bf16[256,128]{1,0:T(8,128)(2,1)S(1)} %project.1.tile, bf16[128,16,128]{2,1,0:T(8,128)(2,1)S(1)} %get-tuple-element.8.own, bf16[128,16,128]{2,1,0:T(8,128)(2,1)S(1)} %collective-permute-done.5.other, f32[2048,1]{1,0:T(8,128)S(1)} %copy.23.row_flip, ...), custom_call_target="tpu_custom_call" | custom-call | tf_op jit(solution)/shard_map/whiten/pallas_call | solution.py:300
  81.2 11.8 %all-to-all-start.2 = ((bf16[128,32,128]{2,1,0:T(8,128)(2,1)}), bf16[128,32,128]{2,1,0:T(8,128)(2,1)S(1)}, u32[]{:S(2)}, u32[]{:S(2)}) async-start(bf16[128,32,128]{2,1,0:T(8,128)(2,1)} %whiten.1), calls=%async_computation.2 | async-start | bytes 2097152 | tf_op jit(solution)/shard_map/all_to_all | solution.py:312
  93.0 0.0 copy-start.11
  93.0 0.6 copy-done.11
  93.7 0.1 copy.24
  93.8 0.5 broadcast.215
  94.3 0.0 copy-done.10
  94.3 0.7 reduce.7
  95.0 0.1 reshape_squeeze.3
  95.0 0.1 convert_reduce_fusion
  95.2 0.5 fusion
  95.7 0.0 copy-start.3
  95.7 0.0 copy-start.4
  95.8 0.0 copy-start.6
  95.8 28.2 %all-to-all-done.2.parts = bf16[128,32,128]{2,1,0:T(8,128)(2,1)S(1)} async-done(((bf16[128,32,128]{2,1,0:T(8,128)(2,1)}), bf16[128,32,128]{2,1,0:T(8,128)(2,1)S(1)}, u32[]{:S(2)}, u32[]{:S(2)}) %all-to-all-start.2) | async-done | bytes 1048608 | tf_op jit(solution)/shard_map/all_to_all | solution.py:312
  124.0 0.0 copy-done.3
  124.0 0.0 copy-done.4
  124.0 0.0 copy-done.6
  124.0 0.5 spectrum.1
  124.5 0.6 broadcast_in_dim.24
  125.2 3.3 %all-to-all-start.3 = ((bf16[4,32,256]{2,1,0:T(8,128)(2,1)}), bf16[4,32,256]{2,1,0:T(8,128)(2,1)S(1)}, u32[]{:S(2)}, u32[]{:S(2)}) async-start(bf16[4,32,256]{2,1,0:T(8,128)(2,1)} %broadcast_in_dim.24), calls=%async_computation.3 | async-start | bytes 131072 | tf_op jit(solution)/shard_map/all_to_all | solution.py:333
  128.5 4.4 %all-to-all-done.3 = bf16[4,32,256]{2,1,0:T(8,128)(2,1)S(1)} async-done(((bf16[4,32,256]{2,1,0:T(8,128)(2,1)}), bf16[4,32,256]{2,1,0:T(8,128)(2,1)S(1)}, u32[]{:S(2)}, u32[]{:S(2)}) %all-to-all-start.3) | async-done | bytes 65568 | tf_op jit(solution)/shard_map/all_to_all | solution.py:333
  132.9 0.2 convolution_convert_fusion
  133.1 0.1 reshape.208
  133.1 20.1 %all_to_all.25 = bf16[128,2,256]{2,1,0:T(2,128)(2,1)S(1)} all-to-all(bf16[128,2,256]{2,1,0:T(2,128)(2,1)S(1)} %reshape.208), channel_id=1, replica_groups=mesh['z'=8,'y'=8,'c'=2,'e'=4] {'z','y','c'}, dimensions={0} | all-to-all | bytes 262144 | tf_op jit(solution)/shard_map/all_to_all | solution.py:343
  153.2 0.8 bitcast_convert_fusion
  (19 shorter events, 0.2 us)
Async XLA Ops:
  0.0 28.9 %copy-start = (s32[1,4,2048]{2,1,0:T(4,128)S(1)}, s32[1,4,2048]{2,1,0:T(4,128)}, u32[]{:S(2)}) copy-start(s32[1,4,2048]{2,1,0:T(4,128)} %param.17) | copy-start | bytes 98308
  0.0 29.4 %collective-permute-start = (bf16[1,16,2048]{2,1,0:T(8,128)(2,1)}, bf16[1,16,2048]{2,1,0:T(8,128)(2,1)S(1)}, u32[]{:S(2)}, u32[]{:S(2)}) collective-permute-start(bf16[1,16,2048]{2,1,0:T(8,128)(2,1)} %bitcast.16), channel_id=1, source_target_pairs={{0,8},{8,16},{16,24},{24,32},{32,40},{40,48},{48,56},{56,0},{1,9},... | collective-permute-start | bytes 196616 | tf_op jit(solution)/shard_map/ppermute | solution.py:246
  4.2 25.3 %collective-permute-start.1 = (bf16[1,16,2048]{2,1,0:T(8,128)(2,1)}, bf16[1,16,2048]{2,1,0:T(8,128)(2,1)S(1)}, u32[]{:S(2)}, u32[]{:S(2)}) collective-permute-start(bf16[1,16,2048]{2,1,0:T(8,128)(2,1)} %bitcast.17), channel_id=1, source_target_pairs={{0,56},{8,0},{16,8},{24,16},{32,24},{40,32},{48,40},{56,48},{1,57}... | collective-permute-start | bytes 196616 | tf_op jit(solution)/shard_map/ppermute | solution.py:246
  8.0 0.7 copy-start.7
  8.7 0.7 copy-start.8
  10.4 40.4 %all-to-all-start = ((bf16[128,8,128]{2,1,0:T(8,128)(2,1)}), bf16[128,8,128]{2,1,0:T(8,128)(2,1)S(1)}, u32[]{:S(2)}, u32[]{:S(2)}) async-start(bf16[128,8,128]{2,1,0:T(8,128)(2,1)} %deal.1), calls=%async_computation | async-start | bytes 524288 | tf_op jit(solution)/shard_map/all_to_all | solution.py:264
  29.0 0.8 copy-start.9
  29.9 20.9 %collective-permute-start.2 = (bf16[3,16,2048]{2,1,0:T(8,128)(2,1)S(1)}, bf16[3,16,2048]{2,1,0:T(8,128)(2,1)S(1)}, u32[]{:S(2)}, u32[]{:S(2)}) collective-permute-start(bf16[3,16,2048]{2,1,0:T(8,128)(2,1)S(1)} %pad_maximum_fusion), channel_id=1, source_target_pairs={{0,24},{8,32},{16,40},{24,48},{32,56},{40,0},{48,8},{56,16},{1,25}... | collective-permute-start | bytes 589832 | tf_op jit(solution)/shard_map/ppermute | solution.py:246
  35.0 21.0 %collective-permute-start.3 = (bf16[2,16,2048]{2,1,0:T(8,128)(2,1)S(1)}, bf16[2,16,2048]{2,1,0:T(8,128)(2,1)S(1)}, u32[]{:S(2)}, u32[]{:S(2)}) collective-permute-start(bf16[2,16,2048]{2,1,0:T(8,128)(2,1)S(1)} %pad_maximum_fusion.1), channel_id=1, source_target_pairs={{0,40},{8,48},{16,56},{24,0},{32,8},{40,16},{48,24},{56,32},{1,41}... | collective-permute-start | bytes 393224 | tf_op jit(solution)/shard_map/ppermute | solution.py:246
  51.9 18.0 %all-to-all-start.1 = ((bf16[4,128,8,128]{3,2,1,0:T(8,128)(2,1)}), bf16[4,128,8,128]{3,2,1,0:T(8,128)(2,1)S(1)}, u32[]{:S(2)}, u32[]{:S(2)}) async-start(bf16[4,128,8,128]{3,2,1,0:T(8,128)(2,1)} %broadcast_in_dim.21), calls=%async_computation.1 | async-start | bytes 2097152 | tf_op jit(solution)/shard_map/all_to_all | solution.py:265
  56.0 19.2 %collective-permute-start.4 = (bf16[8,16,2048]{2,1,0:T(8,128)(2,1)S(1)}, bf16[8,16,2048]{2,1,0:T(8,128)(2,1)S(1)}, u32[]{:S(2)}, u32[]{:S(2)}) collective-permute-start(bf16[8,16,2048]{2,1,0:T(8,128)(2,1)S(1)} %constant_dynamic-update-slice_fusion.own), channel_id=1, source_target_pairs={{0,4},{4,0},{1,5},{5,1},{2,6},{6,2},{3,7},{7,3},{8,12},{12,8},{9,1... | collective-permute-start | bytes 1572872 | tf_op jit(solution)/shard_map/ppermute | solution.py:271
  71.0 5.5 %collective-permute-start.5 = (bf16[128,16,128]{2,1,0:T(8,128)(2,1)S(1)}, bf16[128,16,128]{2,1,0:T(8,128)(2,1)S(1)}, u32[]{:S(2)}, u32[]{:S(2)}) collective-permute-start(bf16[128,16,128]{2,1,0:T(8,128)(2,1)S(1)} %get-tuple-element.8.own), channel_id=1, source_target_pairs={{0,4},{4,0},{1,5},{5,1},{2,6},{6,2},{3,7},{7,3},{8,12},{12,8},{9,1... | collective-permute-start | bytes 1572872 | tf_op jit(solution)/shard_map/ppermute | solution.py:281
  75.3 1.3 copy-start.1
  75.3 1.3 copy-start.2
  75.3 1.3 copy-start.5
  81.2 13.1 %copy-start.10 = (s32[1,1,4,32,1]{3,4,2,1,0:T(1,128)S(1)}, s32[1,1,4,32,1]{3,4,2,1,0:T(1,128)}, u32[]{:S(2)}) copy-start(s32[1,1,4,32,1]{3,4,2,1,0:T(1,128)} %param.19) | copy-start | bytes 1540
  81.2 42.8 %all-to-all-start.2 = ((bf16[128,32,128]{2,1,0:T(8,128)(2,1)}), bf16[128,32,128]{2,1,0:T(8,128)(2,1)S(1)}, u32[]{:S(2)}, u32[]{:S(2)}) async-start(bf16[128,32,128]{2,1,0:T(8,128)(2,1)} %whiten.1), calls=%async_computation.2 | async-start | bytes 2097152 | tf_op jit(solution)/shard_map/all_to_all | solution.py:312
  93.0 0.7 copy-start.11
  95.7 28.3 %copy-start.3 = (bf16[256,256]{1,0:T(8,128)(2,1)S(1)}, bf16[256,256]{1,0:T(8,128)(2,1)}, u32[]{:S(2)}) copy-start(bf16[256,256]{1,0:T(8,128)(2,1)} %constant.85.clone.high) | copy-start | bytes 393220
  95.7 28.3 %copy-start.4 = (bf16[256,256]{1,0:T(8,128)(2,1)S(1)}, bf16[256,256]{1,0:T(8,128)(2,1)}, u32[]{:S(2)}) copy-start(bf16[256,256]{1,0:T(8,128)(2,1)} %constant.86.clone.low) | copy-start | bytes 393220
  95.8 28.2 %copy-start.6 = (f32[2,16,1,128]{3,2,1,0:T(1,128)S(1)}, f32[2,16,1,128]{3,2,1,0:T(1,128)}, u32[]{:S(2)}) copy-start(f32[2,16,1,128]{3,2,1,0:T(1,128)} %constant.84.clone.turns) | copy-start | bytes 49156
  125.2 7.7 %all-to-all-start.3 = ((bf16[4,32,256]{2,1,0:T(8,128)(2,1)}), bf16[4,32,256]{2,1,0:T(8,128)(2,1)S(1)}, u32[]{:S(2)}, u32[]{:S(2)}) async-start(bf16[4,32,256]{2,1,0:T(8,128)(2,1)} %broadcast_in_dim.24), calls=%async_computation.3 | async-start | bytes 131072 | tf_op jit(solution)/shard_map/all_to_all | solution.py:333
where the time goes:
time: 155 us; the launch traced here: 154 us
  starting transfers between devices  60.1 us (39%)
  waiting for transfers between devices  56.3 us (36%)
  blocking collectives  20.1 us (13%)
  Pallas kernels  8.24 us (5%)
  local copies, waits for them, and re-layouts  5.58 us (4%)
  other arithmetic  3.18 us (2%)
    all_to_all x1, waiting for transfers between devices, shards(): partial_rows = lax.all_to_all(partial_cols, ROW_AXES, 0, 0, tiled=True)  28.2 us
    all_to_all x1, blocking collectives, shards(): arrived = lax.all_to_all(outgoing, ROW_AXES, 0, 0, tiled=True)  20.1 us
    all_to_all x1, starting transfers between devices, shards(): pieces = lax.all_to_all(pieces, ROW_AXES, 0, 0, tiled=True)  17.6 us
    ppermute x4, starting transfers between devices, shift_y(): return lax.ppermute(rows, 'y', [(i, (i + step) % NY) for i in range(NY)])  16.3 us
    ppermute x4, waiting for transfers between devices, shift_y(): return lax.ppermute(rows, 'y', [(i, (i + step) % NY) for i in range(NY)])  12.6 us
    all_to_all x1, starting transfers between devices, shards(): partial_rows = lax.all_to_all(partial_cols, ROW_AXES, 0, 0, tiled=True)  11.8 us
    all_to_all x1, waiting for transfers between devices, shards(): lax.all_to_all(jnp.broadcast_to(pieces[None], (NE,) + pieces.shape), 'e',...  10.8 us
    pallas_call x1, Pallas kernels, shards(): pl.pallas_call(whiten_kernel, out_shape=pltpu.VMEM((ROWS, 2 * GROUP_ROWS,...  4.61 us
  transfers between devices with their start and end apart: 10, of which 5 were waited for; matrix products, arithmetic and copies ran while one was open for 3% of the time, Pallas kernels for 2%

commit v1 on v0

--- a/solution.py
+++ b/solution.py
@@ -262,12 +262,14 @@
         name="deal",
     )(right_inv, left_inv)
     pieces = lax.all_to_all(pieces, ROW_AXES, 0, 0, tiled=True)
-    pieces = lax.all_to_all(jnp.broadcast_to(pieces[None], (NE,) + pieces.shape), "e", 0, 0, tiled=True)
+    pieces = jnp.broadcast_to(pieces[None], (NE,) + pieces.shape)
+    pieces = lax.all_to_all(pieces, "e", 0, 0, tiled=True)
 
     swap = [(0, 1), (1, 0)]
     mine = grads.reshape(1, GROUP_ROWS, DM)
     near_rows = jnp.concatenate([shift_y(mine, 1), mine, shift_y(mine, -1)])
-    rows_own = jnp.concatenate([shift_y(near_rows, 3), near_rows, shift_y(near_rows[:2], -3)])
+    far_up, far_down = shift_y(near_rows, 3), shift_y(near_rows[:2], -3)
+    rows_own = jnp.concatenate([far_up, near_rows, far_down])
     rows_other = lax.ppermute(rows_own, "c", swap)
     factor_shape = pltpu.VMEM((ROWS, GROUP_ROWS, BLOCK), bf16)
     right_cols, left_own = pl.pallas_call(

time: 155 us -> 155 us (level)
  no operation moved by 1% of the time
where the time goes in v1:
time: 155 us; the launch traced here: 154 us
  starting transfers between devices  60.1 us (39%)
  waiting for transfers between devices  56.3 us (36%)
  blocking collectives  20.1 us (13%)
  Pallas kernels  8.24 us (5%)
  local copies, waits for them, and re-layouts  5.58 us (4%)
  other arithmetic  3.18 us (2%)
    all_to_all x1, waiting for transfers between devices, shards(): partial_rows = lax.all_to_all(partial_cols, ROW_AXES, 0, 0, tiled=True)  28.2 us
    all_to_all x1, blocking collectives, shards(): arrived = lax.all_to_all(outgoing, ROW_AXES, 0, 0, tiled=True)  20.1 us
    all_to_all x1, starting transfers between devices, shards(): pieces = lax.all_to_all(pieces, ROW_AXES, 0, 0, tiled=True)  17.6 us
    ppermute x4, starting transfers between devices, shift_y(): return lax.ppermute(rows, 'y', [(i, (i + step) % NY) for i in range(NY)])  16.3 us
    ppermute x4, waiting for transfers between devices, shift_y(): return lax.ppermute(rows, 'y', [(i, (i + step) % NY) for i in range(NY)])  12.6 us
    all_to_all x1, starting transfers between devices, shards(): partial_rows = lax.all_to_all(partial_cols, ROW_AXES, 0, 0, tiled=True)  11.8 us
    all_to_all x1, waiting for transfers between devices, shards(): pieces = lax.all_to_all(pieces, 'e', 0, 0, tiled=True)  10.8 us
    pallas_call x1, Pallas kernels, shards(): pl.pallas_call(whiten_kernel, out_shape=pltpu.VMEM((ROWS, 2 * GROUP_ROWS,...  4.61 us
  transfers between devices with their start and end apart: 10, of which 5 were waited for; matrix products, arithmetic and copies ran while one was open for 3% of the time, Pallas kernels for 2%

profile of v1, /device:TPU:1, one launch (start us, length us, event | category | flops | bytes accessed | tf_op | source)
XLA Modules:
  0.0 154.0 jit_solution(2121408312941885918)
XLA Ops:
  0.0 0.0 copy-start
  0.0 4.1 %collective-permute-start = (bf16[1,16,2048]{2,1,0:T(8,128)(2,1)}, bf16[1,16,2048]{2,1,0:T(8,128)(2,1)S(1)}, u32[]{:S(2)}, u32[]{:S(2)}) collective-permute-start(bf16[1,16,2048]{2,1,0:T(8,128)(2,1)} %bitcast.16), channel_id=1, source_target_pairs={{0,8},{8,16},{16,24},{24,32},{32,40},{40,48},{48,56},{56,0},{1,9},... | collective-permute-start | bytes 196616 | tf_op jit(solution)/shard_map/ppermute | solution.py:246
  4.2 3.8 %collective-permute-start.1 = (bf16[1,16,2048]{2,1,0:T(8,128)(2,1)}, bf16[1,16,2048]{2,1,0:T(8,128)(2,1)S(1)}, u32[]{:S(2)}, u32[]{:S(2)}) collective-permute-start(bf16[1,16,2048]{2,1,0:T(8,128)(2,1)} %bitcast.17), channel_id=1, source_target_pairs={{0,56},{8,0},{16,8},{24,16},{32,24},{40,32},{48,40},{56,48},{1,57}... | collective-permute-start | bytes 196616 | tf_op jit(solution)/shard_map/ppermute | solution.py:246
  8.0 0.0 copy-start.7
  8.0 0.7 copy-done.7
  8.7 0.7 copy-done.8
  9.4 1.0 deal.1
  10.4 17.6 %all-to-all-start = ((bf16[128,8,128]{2,1,0:T(8,128)(2,1)}), bf16[128,8,128]{2,1,0:T(8,128)(2,1)S(1)}, u32[]{:S(2)}, u32[]{:S(2)}) async-start(bf16[128,8,128]{2,1,0:T(8,128)(2,1)} %deal.1), calls=%async_computation | async-start | bytes 524288 | tf_op jit(solution)/shard_map/all_to_all | solution.py:264
  28.1 0.8 convert_bitcast_fusion
  28.9 0.0 copy-done
  28.9 0.1 reshape.206
  29.0 0.0 copy-start.9
  29.0 0.4 copy.23.row_flip
  29.4 0.0 collective-permute-done
  29.4 0.0 collective-permute-done.1
  29.4 0.4 copy-done.9
  29.9 5.1 %collective-permute-start.2 = (bf16[3,16,2048]{2,1,0:T(8,128)(2,1)S(1)}, bf16[3,16,2048]{2,1,0:T(8,128)(2,1)S(1)}, u32[]{:S(2)}, u32[]{:S(2)}) collective-permute-start(bf16[3,16,2048]{2,1,0:T(8,128)(2,1)S(1)} %pad_maximum_fusion), channel_id=1, source_target_pairs={{0,24},{8,32},{16,40},{24,48},{32,56},{40,0},{48,8},{56,16},{1,25}... | collective-permute-start | bytes 589832 | tf_op jit(solution)/shard_map/ppermute | solution.py:246
  35.0 3.2 %collective-permute-start.3 = (bf16[2,16,2048]{2,1,0:T(8,128)(2,1)S(1)}, bf16[2,16,2048]{2,1,0:T(8,128)(2,1)S(1)}, u32[]{:S(2)}, u32[]{:S(2)}) collective-permute-start(bf16[2,16,2048]{2,1,0:T(8,128)(2,1)S(1)} %pad_maximum_fusion.1), channel_id=1, source_target_pairs={{0,40},{8,48},{16,56},{24,0},{32,8},{40,16},{48,24},{56,32},{1,41}... | collective-permute-start | bytes 393224 | tf_op jit(solution)/shard_map/ppermute | solution.py:246
  38.2 12.6 %collective-permute-done.2 = bf16[3,16,2048]{2,1,0:T(8,128)(2,1)S(1)} collective-permute-done((bf16[3,16,2048]{2,1,0:T(8,128)(2,1)S(1)}, bf16[3,16,2048]{2,1,0:T(8,128)(2,1)S(1)}, u32[]{:S(2)}, u32[]{:S(2)}) %collective-permute-start.2) | collective-permute-done | bytes 196640 | tf_op jit(solution)/shard_map/ppermute | solution.py:246
  50.8 0.0 all-to-all-done
  50.8 1.1 broadcast_in_dim.21
  51.9 4.0 %all-to-all-start.1 = ((bf16[4,128,8,128]{3,2,1,0:T(8,128)(2,1)}), bf16[4,128,8,128]{3,2,1,0:T(8,128)(2,1)S(1)}, u32[]{:S(2)}, u32[]{:S(2)}) async-start(bf16[4,128,8,128]{3,2,1,0:T(8,128)(2,1)} %broadcast_in_dim.21), calls=%async_computation.1 | async-start | bytes 2097152 | tf_op jit(solution)/shard_map/all_to_all | solution.py:266
  56.0 0.0 collective-permute-done.3
  56.0 3.1 %collective-permute-start.4 = (bf16[8,16,2048]{2,1,0:T(8,128)(2,1)S(1)}, bf16[8,16,2048]{2,1,0:T(8,128)(2,1)S(1)}, u32[]{:S(2)}, u32[]{:S(2)}) collective-permute-start(bf16[8,16,2048]{2,1,0:T(8,128)(2,1)S(1)} %constant_dynamic-update-slice_fusion.own), channel_id=1, source_target_pairs={{0,4},{4,0},{1,5},{5,1},{2,6},{6,2},{3,7},{7,3},{8,12},{12,8},{9,1... | collective-permute-start | bytes 1572872 | tf_op jit(solution)/shard_map/ppermute | solution.py:273
  59.1 10.8 %all-to-all-done.1.pieces = bf16[4,128,8,128]{3,2,1,0:T(8,128)(2,1)S(1)} async-done(((bf16[4,128,8,128]{3,2,1,0:T(8,128)(2,1)}), bf16[4,128,8,128]{3,2,1,0:T(8,128)(2,1)S(1)}, u32[]{:S(2)}, u32[]{:S(2)}) %all-to-all-start.1) | async-done | bytes 1048608 | tf_op jit(solution)/shard_map/all_to_all | solution.py:266
  69.9 1.1 arrange.1
  71.0 4.0 %collective-permute-start.5 = (bf16[128,16,128]{2,1,0:T(8,128)(2,1)S(1)}, bf16[128,16,128]{2,1,0:T(8,128)(2,1)S(1)}, u32[]{:S(2)}, u32[]{:S(2)}) collective-permute-start(bf16[128,16,128]{2,1,0:T(8,128)(2,1)S(1)} %get-tuple-element.8.own), channel_id=1, source_target_pairs={{0,4},{4,0},{1,5},{5,1},{2,6},{6,2},{3,7},{7,3},{8,12},{12,8},{9,1... | collective-permute-start | bytes 1572872 | tf_op jit(solution)/shard_map/ppermute | solution.py:283
  75.0 0.1 pad_add_fusion.place
  75.1 0.1 select_reduce_fusion
  75.2 0.0 collective-permute-done.4.other
  75.3 0.0 copy-start.1
  75.3 0.0 copy-start.2
  75.3 0.0 copy-start.5
  75.3 1.0 project.1.tile
  76.3 0.3 collective-permute-done.5.other
  76.5 0.0 copy-done.1
  76.6 0.0 copy-done.2
  76.6 0.0 copy-done.5
  76.6 4.6 %whiten.1 = bf16[128,32,128]{2,1,0:T(8,128)(2,1)} custom-call(s32[2]{0:T(128)S(1)} %pad_add_fusion.place, bf16[256,128]{1,0:T(8,128)(2,1)S(1)} %project.1.tile, bf16[128,16,128]{2,1,0:T(8,128)(2,1)S(1)} %get-tuple-element.8.own, bf16[128,16,128]{2,1,0:T(8,128)(2,1)S(1)} %collective-permute-done.5.other, f32[2048,1]{1,0:T(8,128)S(1)} %copy.23.row_flip, ...), custom_call_target="tpu_custom_call" | custom-call | tf_op jit(solution)/shard_map/whiten/pallas_call | solution.py:302
  81.2 11.8 %all-to-all-start.2 = ((bf16[128,32,128]{2,1,0:T(8,128)(2,1)}), bf16[128,32,128]{2,1,0:T(8,128)(2,1)S(1)}, u32[]{:S(2)}, u32[]{:S(2)}) async-start(bf16[128,32,128]{2,1,0:T(8,128)(2,1)} %whiten.1), calls=%async_computation.2 | async-start | bytes 2097152 | tf_op jit(solution)/shard_map/all_to_all | solution.py:314
  93.0 0.0 copy-start.11
  93.0 0.6 copy-done.11
  93.7 0.1 copy.24
  93.8 0.5 broadcast.215
  94.3 0.0 copy-done.10
  94.3 0.7 reduce.7
  95.0 0.1 reshape_squeeze.3
  95.0 0.1 convert_reduce_fusion
  95.2 0.5 fusion
  95.7 0.0 copy-start.3
  95.7 0.0 copy-start.4
  95.8 0.0 copy-start.6
  95.8 28.2 %all-to-all-done.2.parts = bf16[128,32,128]{2,1,0:T(8,128)(2,1)S(1)} async-done(((bf16[128,32,128]{2,1,0:T(8,128)(2,1)}), bf16[128,32,128]{2,1,0:T(8,128)(2,1)S(1)}, u32[]{:S(2)}, u32[]{:S(2)}) %all-to-all-start.2) | async-done | bytes 1048608 | tf_op jit(solution)/shard_map/all_to_all | solution.py:314
  124.0 0.0 copy-done.3
  124.0 0.0 copy-done.4
  124.0 0.0 copy-done.6
  124.0 0.5 spectrum.1
  124.5 0.6 broadcast_in_dim.24
  125.2 3.3 %all-to-all-start.3 = ((bf16[4,32,256]{2,1,0:T(8,128)(2,1)}), bf16[4,32,256]{2,1,0:T(8,128)(2,1)S(1)}, u32[]{:S(2)}, u32[]{:S(2)}) async-start(bf16[4,32,256]{2,1,0:T(8,128)(2,1)} %broadcast_in_dim.24), calls=%async_computation.3 | async-start | bytes 131072 | tf_op jit(solution)/shard_map/all_to_all | solution.py:335
  128.5 4.4 %all-to-all-done.3 = bf16[4,32,256]{2,1,0:T(8,128)(2,1)S(1)} async-done(((bf16[4,32,256]{2,1,0:T(8,128)(2,1)}), bf16[4,32,256]{2,1,0:T(8,128)(2,1)S(1)}, u32[]{:S(2)}, u32[]{:S(2)}) %all-to-all-start.3) | async-done | bytes 65568 | tf_op jit(solution)/shard_map/all_to_all | solution.py:335
  132.9 0.2 convolution_convert_fusion
  133.1 0.1 reshape.208
  133.1 20.1 %all_to_all.25 = bf16[128,2,256]{2,1,0:T(2,128)(2,1)S(1)} all-to-all(bf16[128,2,256]{2,1,0:T(2,128)(2,1)S(1)} %reshape.208), channel_id=1, replica_groups=mesh['z'=8,'y'=8,'c'=2,'e'=4] {'z','y','c'}, dimensions={0} | all-to-all | bytes 262144 | tf_op jit(solution)/shard_map/all_to_all | solution.py:345
  153.2 0.8 bitcast_convert_fusion
  (19 shorter events, 0.2 us)
Async XLA Ops:
  0.0 28.9 %copy-start = (s32[1,4,2048]{2,1,0:T(4,128)S(1)}, s32[1,4,2048]{2,1,0:T(4,128)}, u32[]{:S(2)}) copy-start(s32[1,4,2048]{2,1,0:T(4,128)} %param.17) | copy-start | bytes 98308
  0.0 29.4 %collective-permute-start = (bf16[1,16,2048]{2,1,0:T(8,128)(2,1)}, bf16[1,16,2048]{2,1,0:T(8,128)(2,1)S(1)}, u32[]{:S(2)}, u32[]{:S(2)}) collective-permute-start(bf16[1,16,2048]{2,1,0:T(8,128)(2,1)} %bitcast.16), channel_id=1, source_target_pairs={{0,8},{8,16},{16,24},{24,32},{32,40},{40,48},{48,56},{56,0},{1,9},... | collective-permute-start | bytes 196616 | tf_op jit(solution)/shard_map/ppermute | solution.py:246
  4.2 25.3 %collective-permute-start.1 = (bf16[1,16,2048]{2,1,0:T(8,128)(2,1)}, bf16[1,16,2048]{2,1,0:T(8,128)(2,1)S(1)}, u32[]{:S(2)}, u32[]{:S(2)}) collective-permute-start(bf16[1,16,2048]{2,1,0:T(8,128)(2,1)} %bitcast.17), channel_id=1, source_target_pairs={{0,56},{8,0},{16,8},{24,16},{32,24},{40,32},{48,40},{56,48},{1,57}... | collective-permute-start | bytes 196616 | tf_op jit(solution)/shard_map/ppermute | solution.py:246
  8.0 0.7 copy-start.7
  8.7 0.7 copy-start.8
  10.4 40.4 %all-to-all-start = ((bf16[128,8,128]{2,1,0:T(8,128)(2,1)}), bf16[128,8,128]{2,1,0:T(8,128)(2,1)S(1)}, u32[]{:S(2)}, u32[]{:S(2)}) async-start(bf16[128,8,128]{2,1,0:T(8,128)(2,1)} %deal.1), calls=%async_computation | async-start | bytes 524288 | tf_op jit(solution)/shard_map/all_to_all | solution.py:264
  29.0 0.8 copy-start.9
  29.9 20.9 %collective-permute-start.2 = (bf16[3,16,2048]{2,1,0:T(8,128)(2,1)S(1)}, bf16[3,16,2048]{2,1,0:T(8,128)(2,1)S(1)}, u32[]{:S(2)}, u32[]{:S(2)}) collective-permute-start(bf16[3,16,2048]{2,1,0:T(8,128)(2,1)S(1)} %pad_maximum_fusion), channel_id=1, source_target_pairs={{0,24},{8,32},{16,40},{24,48},{32,56},{40,0},{48,8},{56,16},{1,25}... | collective-permute-start | bytes 589832 | tf_op jit(solution)/shard_map/ppermute | solution.py:246
  35.0 21.0 %collective-permute-start.3 = (bf16[2,16,2048]{2,1,0:T(8,128)(2,1)S(1)}, bf16[2,16,2048]{2,1,0:T(8,128)(2,1)S(1)}, u32[]{:S(2)}, u32[]{:S(2)}) collective-permute-start(bf16[2,16,2048]{2,1,0:T(8,128)(2,1)S(1)} %pad_maximum_fusion.1), channel_id=1, source_target_pairs={{0,40},{8,48},{16,56},{24,0},{32,8},{40,16},{48,24},{56,32},{1,41}... | collective-permute-start | bytes 393224 | tf_op jit(solution)/shard_map/ppermute | solution.py:246
  51.9 18.0 %all-to-all-start.1 = ((bf16[4,128,8,128]{3,2,1,0:T(8,128)(2,1)}), bf16[4,128,8,128]{3,2,1,0:T(8,128)(2,1)S(1)}, u32[]{:S(2)}, u32[]{:S(2)}) async-start(bf16[4,128,8,128]{3,2,1,0:T(8,128)(2,1)} %broadcast_in_dim.21), calls=%async_computation.1 | async-start | bytes 2097152 | tf_op jit(solution)/shard_map/all_to_all | solution.py:266
  56.0 19.2 %collective-permute-start.4 = (bf16[8,16,2048]{2,1,0:T(8,128)(2,1)S(1)}, bf16[8,16,2048]{2,1,0:T(8,128)(2,1)S(1)}, u32[]{:S(2)}, u32[]{:S(2)}) collective-permute-start(bf16[8,16,2048]{2,1,0:T(8,128)(2,1)S(1)} %constant_dynamic-update-slice_fusion.own), channel_id=1, source_target_pairs={{0,4},{4,0},{1,5},{5,1},{2,6},{6,2},{3,7},{7,3},{8,12},{12,8},{9,1... | collective-permute-start | bytes 1572872 | tf_op jit(solution)/shard_map/ppermute | solution.py:273
  71.0 5.5 %collective-permute-start.5 = (bf16[128,16,128]{2,1,0:T(8,128)(2,1)S(1)}, bf16[128,16,128]{2,1,0:T(8,128)(2,1)S(1)}, u32[]{:S(2)}, u32[]{:S(2)}) collective-permute-start(bf16[128,16,128]{2,1,0:T(8,128)(2,1)S(1)} %get-tuple-element.8.own), channel_id=1, source_target_pairs={{0,4},{4,0},{1,5},{5,1},{2,6},{6,2},{3,7},{7,3},{8,12},{12,8},{9,1... | collective-permute-start | bytes 1572872 | tf_op jit(solution)/shard_map/ppermute | solution.py:283
  75.3 1.3 copy-start.1
  75.3 1.3 copy-start.2
  75.3 1.3 copy-start.5
  81.2 13.1 %copy-start.10 = (s32[1,1,4,32,1]{3,4,2,1,0:T(1,128)S(1)}, s32[1,1,4,32,1]{3,4,2,1,0:T(1,128)}, u32[]{:S(2)}) copy-start(s32[1,1,4,32,1]{3,4,2,1,0:T(1,128)} %param.19) | copy-start | bytes 1540
  81.2 42.8 %all-to-all-start.2 = ((bf16[128,32,128]{2,1,0:T(8,128)(2,1)}), bf16[128,32,128]{2,1,0:T(8,128)(2,1)S(1)}, u32[]{:S(2)}, u32[]{:S(2)}) async-start(bf16[128,32,128]{2,1,0:T(8,128)(2,1)} %whiten.1), calls=%async_computation.2 | async-start | bytes 2097152 | tf_op jit(solution)/shard_map/all_to_all | solution.py:314
  93.0 0.7 copy-start.11
  95.7 28.3 %copy-start.3 = (bf16[256,256]{1,0:T(8,128)(2,1)S(1)}, bf16[256,256]{1,0:T(8,128)(2,1)}, u32[]{:S(2)}) copy-start(bf16[256,256]{1,0:T(8,128)(2,1)} %constant.85.clone.high) | copy-start | bytes 393220
  95.7 28.3 %copy-start.4 = (bf16[256,256]{1,0:T(8,128)(2,1)S(1)}, bf16[256,256]{1,0:T(8,128)(2,1)}, u32[]{:S(2)}) copy-start(bf16[256,256]{1,0:T(8,128)(2,1)} %constant.86.clone.low) | copy-start | bytes 393220
  95.8 28.2 %copy-start.6 = (f32[2,16,1,128]{3,2,1,0:T(1,128)S(1)}, f32[2,16,1,128]{3,2,1,0:T(1,128)}, u32[]{:S(2)}) copy-start(f32[2,16,1,128]{3,2,1,0:T(1,128)} %constant.84.clone.turns) | copy-start | bytes 49156
  125.2 7.7 %all-to-all-start.3 = ((bf16[4,32,256]{2,1,0:T(8,128)(2,1)}), bf16[4,32,256]{2,1,0:T(8,128)(2,1)S(1)}, u32[]{:S(2)}, u32[]{:S(2)}) async-start(bf16[4,32,256]{2,1,0:T(8,128)(2,1)} %broadcast_in_dim.24), calls=%async_computation.3 | async-start | bytes 131072 | tf_op jit(solution)/shard_map/all_to_all | solution.py:335

commit v2 on v1

--- a/solution.py
+++ b/solution.py
@@ -31,7 +31,12 @@
 def split_table(table):
     high = table.astype(bf16)
     low = (table - high.astype(np.float64)).astype(bf16)
-    return high, low
+    return [high, low]
+
+
+def split_values(values):
+    high = values.astype(bf16)
+    return [high, (values - high.astype(f32)).astype(bf16)]
 
 
 def dft_angles(rows, cols, length):
@@ -43,7 +48,7 @@
     high, low = split_table(np.concatenate([np.cos(angles), -np.sin(angles)], axis=0))
     angles = dft_angles(INNER, RADIX, DM)
     twiddles = np.concatenate([np.cos(angles), -np.sin(angles)], axis=1).astype(np.float32)
-    return high, low, twiddles
+    return np.concatenate([high, low, high], axis=1), twiddles
 
 
 def row_tables():
@@ -55,7 +60,7 @@
     high, low = split_table(full)
     angles = dft_angles(NYC, BLOCK, DM)
     twiddles = np.stack([np.cos(angles), -np.sin(angles)]).astype(np.float32)
-    return high, low, twiddles.reshape(2, NYC, 1, BLOCK)
+    return np.concatenate([high, low, high], axis=0), twiddles.reshape(2, NYC, 1, BLOCK)
 
 
 def add(a, b):
@@ -110,7 +115,15 @@
     return jnp.dot(a, b, preferred_element_type=f32)
 
 
-def deal_kernel(right, left, out):
+def deal_kernel(right_far, left_far, out, right, left, arrived):
+    copies = [
+        pltpu.make_async_copy(right_far, right, arrived.at[0]),
+        pltpu.make_async_copy(left_far, left, arrived.at[1]),
+    ]
+    for copy in copies:
+        copy.start()
+    for copy in copies:
+        copy.wait()
     quarter = GROUP_ROWS // NE
     width = right.shape[1]
     pack = BLOCK // NE
@@ -179,7 +192,7 @@
             out[pl.ds(start, GROUP_ROWS), :] = part[k]
 
 
-def whiten_kernel(place, tile, own, other, row_flip, high, low, twiddles, out, white, stage):
+def whiten_kernel(place, tile, own, other, row_flip, table, twiddles, out, white, stage):
     left = jnp.concatenate([own[...].reshape(DM, BLOCK), other[...].reshape(DM, BLOCK)], axis=1)
     half = TILE_ROWS // NC
     starts = [pl.multiple_of(half * side, half) for side in (place[1], 1 - place[1])]
@@ -188,9 +201,8 @@
     for p in range(0, RADIX, 2):
         pair = [white[pl.ds(p + k, INNER, stride=RADIX), :] for k in range(2)]
         part = jnp.concatenate(pair, axis=1)
-        part_high = part.astype(bf16)
-        part_low = (part - part_high.astype(f32)).astype(bf16)
-        both = dot(high[...], part_high) + dot(low[...], part_high) + dot(high[...], part_low)
+        part_high, part_low = split_values(part)
+        both = dot(table[...], jnp.concatenate([part_high, part_high, part_low], axis=0))
         stage[p] = both[:, 0:BLOCK]
         stage[p + 1] = both[:, BLOCK:]
 
@@ -210,7 +222,7 @@
     lax.fori_loop(0, INNER // GROUP_ROWS, combine, 0, unroll=4)
 
 
-def spectrum_kernel(parts, cross, turns, high, low, wanted, out, mixed):
+def spectrum_kernel(parts, cross, turns, table, wanted, out, mixed):
     for yc in range(NYC):
         total = parts[yc].astype(f32)
         for z in range(1, NZ):
@@ -219,9 +231,8 @@
         mixed[yc, :, 0:BLOCK] = value[0]
         mixed[yc, :, BLOCK : 2 * BLOCK] = value[1]
     rows = mixed[...].reshape(NYC * GROUP_ROWS, 2 * BLOCK)
-    rows_high = rows.astype(bf16)
-    rows_low = (rows - rows_high.astype(f32)).astype(bf16)
-    rows = dot(rows_high, high[...]) + dot(rows_low, high[...]) + dot(rows_high, low[...])
+    rows_high, rows_low = split_values(rows)
+    rows = dot(jnp.concatenate([rows_high, rows_high, rows_low], axis=1), table[...])
     rows = rows.reshape(NYC, GROUP_ROWS, 2 * BLOCK)
     terms = [
         mul((rows[yc, :, 0:BLOCK], rows[yc, :, BLOCK:]), (turns[0, yc], turns[1, yc]))
@@ -255,9 +266,13 @@
 
     pieces = pl.pallas_call(
         deal_kernel,
-        out_shape=pltpu.VMEM((ROWS, 2 * GROUP_ROWS // NE, BLOCK), bf16),
-        in_specs=[IN_VMEM] * 2,
-        out_specs=IN_VMEM,
+        out_shape=jax.ShapeDtypeStruct((ROWS, 2 * GROUP_ROWS // NE, BLOCK), bf16),
+        in_specs=[pl.BlockSpec(memory_space=pl.ANY)] * 2,
+        scratch_shapes=[
+            pltpu.VMEM(right_inv.shape, bf16),
+            pltpu.VMEM(left_inv.shape, bf16),
+            pltpu.SemaphoreType.DMA((2,)),
+        ],
         compiler_params=grant(8),
         name="deal",
     )(right_inv, left_inv)
@@ -290,7 +305,20 @@
     own_col = jnp.arange(NYC, dtype=jnp.int32) == yc_id
     col_bits = jnp.sum(jnp.where(own_col[None, :], col_bits, 0), axis=1)[None, :]
     col_flip = (1 - 2 * col_bits).astype(f32)
-    high, low, twiddles = column_tables()
+    spectrum_rows = row_id * GROUP_ROWS + jnp.arange(GROUP_ROWS, dtype=jnp.int32)
+    columns = jnp.arange(NYC, dtype=jnp.int32)[:, None] + NYC * jnp.arange(BLOCK, dtype=jnp.int32)
+    columns = columns.reshape(NYC, 1, BLOCK)
+    phase = spectrum_rows[None, :, None] * columns
+    angle = phase.astype(f32) * (2.0 * math.pi / (DM * DM))
+    cross = jnp.stack([jnp.cos(angle), -jnp.sin(angle)]) * (1.0 / DM)
+    local_ids = listed[0, 0, 0] - row_id * (GROUP_ROWS * NYC)
+    wanted = (local_ids % NYC) * GROUP_ROWS + local_ids // NYC
+    wanted = wanted[:, None]
+    owner_ids = owners[0, 0, :, :, 0].reshape(-1)
+    order = jnp.arange(NE * list_len, dtype=jnp.int32)
+    same = (owner_ids[:, None] == owner_ids[None, :]) & (order[:, None] < order[None, :])
+    position = owner_ids * capacity + jnp.sum(same.astype(jnp.int32), axis=0)
+    column_table, twiddles = column_tables()
     tile = pl.pallas_call(
         project_kernel,
         out_shape=pltpu.VMEM((TILE_ROWS, BLOCK), bf16),
@@ -302,7 +330,7 @@
     partial_cols = pl.pallas_call(
         whiten_kernel,
         out_shape=pltpu.VMEM((ROWS, 2 * GROUP_ROWS, BLOCK), bf16),
-        in_specs=[IN_SMEM] + [IN_VMEM] * 7,
+        in_specs=[IN_SMEM] + [IN_VMEM] * 6,
         out_specs=IN_VMEM,
         scratch_shapes=[
             pltpu.VMEM((DM, BLOCK), f32),
@@ -310,35 +338,23 @@
         ],
         compiler_params=grant(16),
         name="whiten",
-    )(place, near(tile), near(left_own), near(left_other), row_flip, high, low, twiddles)
+    )(place, near(tile), near(left_own), near(left_other), row_flip, column_table, twiddles)
     partial_rows = lax.all_to_all(partial_cols, ROW_AXES, 0, 0, tiled=True)
 
-    spectrum_rows = row_id * GROUP_ROWS + jnp.arange(GROUP_ROWS, dtype=jnp.int32)
-    columns = jnp.arange(NYC, dtype=jnp.int32)[:, None] + NYC * jnp.arange(BLOCK, dtype=jnp.int32)
-    columns = columns.reshape(NYC, 1, BLOCK)
-    phase = spectrum_rows[None, :, None] * columns
-    angle = phase.astype(f32) * (2.0 * math.pi / (DM * DM))
-    cross = jnp.stack([jnp.cos(angle), -jnp.sin(angle)]) * (1.0 / DM)
-    local_ids = listed[0, 0, 0] - row_id * (GROUP_ROWS * NYC)
-    wanted = (local_ids % NYC) * GROUP_ROWS + local_ids // NYC
-    row_high, row_low, turns = row_tables()
+    row_table, turns = row_tables()
     picked = pl.pallas_call(
         spectrum_kernel,
         out_shape=pltpu.VMEM((list_len, 2 * BLOCK), bf16),
-        in_specs=[IN_VMEM] * 6,
+        in_specs=[IN_VMEM] * 5,
         out_specs=IN_VMEM,
         scratch_shapes=[pltpu.VMEM((NYC, GROUP_ROWS, 2 * BLOCK), f32)],
         compiler_params=grant(12),
         name="spectrum",
-    )(near(partial_rows), near(cross), turns, row_high, row_low, wanted[:, None])
+    )(near(partial_rows), near(cross), turns, row_table, wanted)
 
     entries = lax.all_to_all(
         jnp.broadcast_to(picked[None], (NE,) + picked.shape), "e", 0, 0, tiled=True
     ).reshape(NE * list_len, 2 * BLOCK)
-    owner_ids = owners[0, 0, :, :, 0].reshape(-1)
-    order = jnp.arange(NE * list_len, dtype=jnp.int32)
-    same = (owner_ids[:, None] == owner_ids[None, :]) & (order[:, None] < order[None, :])
-    position = owner_ids * capacity + jnp.sum(same.astype(jnp.int32), axis=0)
     place = jnp.arange(ROWS * capacity, dtype=jnp.int32)[:, None] == position[None, :]
     outgoing = dot(place.astype(bf16), entries).astype(bf16)
     outgoing = outgoing.reshape(ROWS, capacity, 2 * BLOCK)

time: 155 us -> 155 us (level)
    unnamed x29 -> x25, local copies, waits for them, and re-layouts: 3.1 us -> 3.09 us
where the time goes in v2:
time: 155 us; the launch traced here: 154 us
  starting transfers between devices  60.1 us (39%)
  waiting for transfers between devices  56.3 us (36%)
  blocking collectives  20.1 us (13%)
  Pallas kernels  8.26 us (5%)
  local copies, waits for them, and re-layouts  5.57 us (4%)
  other arithmetic  3.18 us (2%)
    all_to_all x1, waiting for transfers between devices, shards(): partial_rows = lax.all_to_all(partial_cols, ROW_AXES, 0, 0, tiled=True)  28.2 us
    all_to_all x1, blocking collectives, shards(): arrived = lax.all_to_all(outgoing, ROW_AXES, 0, 0, tiled=True)  20.1 us
    all_to_all x1, starting transfers between devices, shards(): pieces = lax.all_to_all(pieces, ROW_AXES, 0, 0, tiled=True)  17.6 us
    ppermute x4, starting transfers between devices, shift_y(): return lax.ppermute(rows, 'y', [(i, (i + step) % NY) for i in range(NY)])  16.3 us
    ppermute x4, waiting for transfers between devices, shift_y(): return lax.ppermute(rows, 'y', [(i, (i + step) % NY) for i in range(NY)])  12.6 us
    all_to_all x1, starting transfers between devices, shards(): partial_rows = lax.all_to_all(partial_cols, ROW_AXES, 0, 0, tiled=True)  11.8 us
    all_to_all x1, waiting for transfers between devices, shards(): pieces = lax.all_to_all(pieces, 'e', 0, 0, tiled=True)  10.8 us
    pallas_call x1, Pallas kernels, shards(): pl.pallas_call(whiten_kernel, out_shape=pltpu.VMEM((ROWS, 2 * GROUP_ROWS,...  4.61 us
  transfers between devices with their start and end apart: 10, of which 5 were waited for; matrix products, arithmetic and copies ran while one was open for 3% of the time, Pallas kernels for 2%

profile of v2, /device:TPU:1, one launch (start us, length us, event | category | flops | bytes accessed | tf_op | source)
XLA Modules:
  0.0 154.1 jit_solution(6310728202558164739)
XLA Ops:
  0.0 0.0 copy-start
  0.0 4.1 %collective-permute-start = (bf16[1,16,2048]{2,1,0:T(8,128)(2,1)}, bf16[1,16,2048]{2,1,0:T(8,128)(2,1)S(1)}, u32[]{:S(2)}, u32[]{:S(2)}) collective-permute-start(bf16[1,16,2048]{2,1,0:T(8,128)(2,1)} %bitcast.16), channel_id=1, source_target_pairs={{0,8},{8,16},{16,24},{24,32},{32,40},{40,48},{48,56},{56,0},{1,9},... | collective-permute-start | bytes 196616 | tf_op jit(solution)/shard_map/ppermute | solution.py:257
  4.2 3.8 %collective-permute-start.1 = (bf16[1,16,2048]{2,1,0:T(8,128)(2,1)}, bf16[1,16,2048]{2,1,0:T(8,128)(2,1)S(1)}, u32[]{:S(2)}, u32[]{:S(2)}) collective-permute-start(bf16[1,16,2048]{2,1,0:T(8,128)(2,1)} %bitcast.17), channel_id=1, source_target_pairs={{0,56},{8,0},{16,8},{24,16},{32,24},{40,32},{48,40},{56,48},{1,57}... | collective-permute-start | bytes 196616 | tf_op jit(solution)/shard_map/ppermute | solution.py:257
  8.0 0.0 copy-start.5
  8.0 0.7 copy-done.5
  8.7 0.0 copy-start.6
  8.7 0.7 copy-done.6
  9.4 1.1 deal.1
  10.5 17.6 %all-to-all-start = ((bf16[128,8,128]{2,1,0:T(8,128)(2,1)}), bf16[128,8,128]{2,1,0:T(8,128)(2,1)S(1)}, u32[]{:S(2)}, u32[]{:S(2)}) async-start(bf16[128,8,128]{2,1,0:T(8,128)(2,1)} %deal.1), calls=%async_computation | async-start | bytes 524288 | tf_op jit(solution)/shard_map/all_to_all | solution.py:279
  28.1 0.8 convert_bitcast_fusion
  28.9 0.0 copy-done
  29.0 0.1 reshape.206
  29.1 0.0 copy-start.7
  29.1 0.4 copy.21.row_flip
  29.5 0.0 collective-permute-done
  29.5 0.0 collective-permute-done.1
  29.5 0.4 copy-done.7
  29.9 5.1 %collective-permute-start.2 = (bf16[3,16,2048]{2,1,0:T(8,128)(2,1)S(1)}, bf16[3,16,2048]{2,1,0:T(8,128)(2,1)S(1)}, u32[]{:S(2)}, u32[]{:S(2)}) collective-permute-start(bf16[3,16,2048]{2,1,0:T(8,128)(2,1)S(1)} %pad_maximum_fusion), channel_id=1, source_target_pairs={{0,24},{8,32},{16,40},{24,48},{32,56},{40,0},{48,8},{56,16},{1,25}... | collective-permute-start | bytes 589832 | tf_op jit(solution)/shard_map/ppermute | solution.py:257
  35.0 3.2 %collective-permute-start.3 = (bf16[2,16,2048]{2,1,0:T(8,128)(2,1)S(1)}, bf16[2,16,2048]{2,1,0:T(8,128)(2,1)S(1)}, u32[]{:S(2)}, u32[]{:S(2)}) collective-permute-start(bf16[2,16,2048]{2,1,0:T(8,128)(2,1)S(1)} %pad_maximum_fusion.1), channel_id=1, source_target_pairs={{0,40},{8,48},{16,56},{24,0},{32,8},{40,16},{48,24},{56,32},{1,41}... | collective-permute-start | bytes 393224 | tf_op jit(solution)/shard_map/ppermute | solution.py:257
  38.3 12.6 %collective-permute-done.2 = bf16[3,16,2048]{2,1,0:T(8,128)(2,1)S(1)} collective-permute-done((bf16[3,16,2048]{2,1,0:T(8,128)(2,1)S(1)}, bf16[3,16,2048]{2,1,0:T(8,128)(2,1)S(1)}, u32[]{:S(2)}, u32[]{:S(2)}) %collective-permute-start.2) | collective-permute-done | bytes 196640 | tf_op jit(solution)/shard_map/ppermute | solution.py:257
  50.9 0.0 all-to-all-done
  50.9 1.1 broadcast_in_dim.21
  52.0 4.0 %all-to-all-start.1 = ((bf16[4,128,8,128]{3,2,1,0:T(8,128)(2,1)}), bf16[4,128,8,128]{3,2,1,0:T(8,128)(2,1)S(1)}, u32[]{:S(2)}, u32[]{:S(2)}) async-start(bf16[4,128,8,128]{3,2,1,0:T(8,128)(2,1)} %broadcast_in_dim.21), calls=%async_computation.1 | async-start | bytes 2097152 | tf_op jit(solution)/shard_map/all_to_all | solution.py:281
  56.0 0.0 collective-permute-done.3
  56.1 3.1 %collective-permute-start.4 = (bf16[8,16,2048]{2,1,0:T(8,128)(2,1)S(1)}, bf16[8,16,2048]{2,1,0:T(8,128)(2,1)S(1)}, u32[]{:S(2)}, u32[]{:S(2)}) collective-permute-start(bf16[8,16,2048]{2,1,0:T(8,128)(2,1)S(1)} %constant_dynamic-update-slice_fusion.own), channel_id=1, source_target_pairs={{0,4},{4,0},{1,5},{5,1},{2,6},{6,2},{3,7},{7,3},{8,12},{12,8},{9,1... | collective-permute-start | bytes 1572872 | tf_op jit(solution)/shard_map/ppermute | solution.py:288
  59.2 10.8 %all-to-all-done.1.pieces = bf16[4,128,8,128]{3,2,1,0:T(8,128)(2,1)S(1)} async-done(((bf16[4,128,8,128]{3,2,1,0:T(8,128)(2,1)}), bf16[4,128,8,128]{3,2,1,0:T(8,128)(2,1)S(1)}, u32[]{:S(2)}, u32[]{:S(2)}) %all-to-all-start.1) | async-done | bytes 1048608 | tf_op jit(solution)/shard_map/all_to_all | solution.py:281
  70.0 1.1 arrange.1
  71.1 4.0 %collective-permute-start.5 = (bf16[128,16,128]{2,1,0:T(8,128)(2,1)S(1)}, bf16[128,16,128]{2,1,0:T(8,128)(2,1)S(1)}, u32[]{:S(2)}, u32[]{:S(2)}) collective-permute-start(bf16[128,16,128]{2,1,0:T(8,128)(2,1)S(1)} %get-tuple-element.8.own), channel_id=1, source_target_pairs={{0,4},{4,0},{1,5},{5,1},{2,6},{6,2},{3,7},{7,3},{8,12},{12,8},{9,1... | collective-permute-start | bytes 1572872 | tf_op jit(solution)/shard_map/ppermute | solution.py:298
  75.1 0.1 pad_add_fusion.place
  75.2 0.1 select_reduce_fusion
  75.3 0.0 collective-permute-done.4.other
  75.3 0.0 copy-start.1
  75.3 0.0 copy-start.3
  75.3 1.0 project.1.tile
  76.3 0.3 collective-permute-done.5.other
  76.6 0.0 copy-done.1
  76.6 0.0 copy-done.3
  76.6 4.6 %whiten.1 = bf16[128,32,128]{2,1,0:T(8,128)(2,1)} custom-call(s32[2]{0:T(128)S(1)} %pad_add_fusion.place, bf16[256,128]{1,0:T(8,128)(2,1)S(1)} %project.1.tile, bf16[128,16,128]{2,1,0:T(8,128)(2,1)S(1)} %get-tuple-element.8.own, bf16[128,16,128]{2,1,0:T(8,128)(2,1)S(1)} %collective-permute-done.5.other, f32[2048,1]{1,0:T(8,128)S(1)} %copy.21.row_flip, ...), custom_call_target="tpu_custom_call" | custom-call | tf_op jit(solution)/shard_map/whiten/pallas_call | solution.py:330
  81.2 0.0 copy-start.8
  81.2 11.8 %all-to-all-start.2 = ((bf16[128,32,128]{2,1,0:T(8,128)(2,1)}), bf16[128,32,128]{2,1,0:T(8,128)(2,1)S(1)}, u32[]{:S(2)}, u32[]{:S(2)}) async-start(bf16[128,32,128]{2,1,0:T(8,128)(2,1)} %whiten.1), calls=%async_computation.2 | async-start | bytes 2097152 | tf_op jit(solution)/shard_map/all_to_all | solution.py:342
  93.1 0.0 copy-start.9
  93.1 0.6 copy-done.9
  93.7 0.1 copy.22
  93.8 0.5 broadcast.215
  94.3 0.0 copy-done.8
  94.3 0.7 reduce.7
  95.0 0.1 reshape_squeeze.3
  95.1 0.1 convert_reduce_fusion
  95.2 0.0 copy-start.2
  95.2 0.5 fusion
  95.8 0.0 copy-start.4
  95.8 28.2 %all-to-all-done.2.parts = bf16[128,32,128]{2,1,0:T(8,128)(2,1)S(1)} async-done(((bf16[128,32,128]{2,1,0:T(8,128)(2,1)}), bf16[128,32,128]{2,1,0:T(8,128)(2,1)S(1)}, u32[]{:S(2)}, u32[]{:S(2)}) %all-to-all-start.2) | async-done | bytes 1048608 | tf_op jit(solution)/shard_map/all_to_all | solution.py:342
  124.0 0.0 copy-done.2
  124.0 0.0 copy-done.4
  124.0 0.5 spectrum.1
  124.6 0.6 broadcast_in_dim.24
  125.2 3.3 %all-to-all-start.3 = ((bf16[4,32,256]{2,1,0:T(8,128)(2,1)}), bf16[4,32,256]{2,1,0:T(8,128)(2,1)S(1)}, u32[]{:S(2)}, u32[]{:S(2)}) async-start(bf16[4,32,256]{2,1,0:T(8,128)(2,1)} %broadcast_in_dim.24), calls=%async_computation.3 | async-start | bytes 131072 | tf_op jit(solution)/shard_map/all_to_all | solution.py:355
  128.5 4.4 %all-to-all-done.3 = bf16[4,32,256]{2,1,0:T(8,128)(2,1)S(1)} async-done(((bf16[4,32,256]{2,1,0:T(8,128)(2,1)}), bf16[4,32,256]{2,1,0:T(8,128)(2,1)S(1)}, u32[]{:S(2)}, u32[]{:S(2)}) %all-to-all-start.3) | async-done | bytes 65568 | tf_op jit(solution)/shard_map/all_to_all | solution.py:355
  132.9 0.2 convolution_convert_fusion
  133.1 0.1 reshape.208
  133.2 20.1 %all_to_all.25 = bf16[128,2,256]{2,1,0:T(2,128)(2,1)S(1)} all-to-all(bf16[128,2,256]{2,1,0:T(2,128)(2,1)S(1)} %reshape.208), channel_id=1, replica_groups=mesh['z'=8,'y'=8,'c'=2,'e'=4] {'z','y','c'}, dimensions={0} | all-to-all | bytes 262144 | tf_op jit(solution)/shard_map/all_to_all | solution.py:361
  153.3 0.8 bitcast_convert_fusion
  (17 shorter events, 0.2 us)
Async XLA Ops:
  0.0 28.9 %copy-start = (s32[1,4,2048]{2,1,0:T(4,128)S(1)}, s32[1,4,2048]{2,1,0:T(4,128)}, u32[]{:S(2)}) copy-start(s32[1,4,2048]{2,1,0:T(4,128)} %param.15) | copy-start | bytes 98308
  0.0 29.4 %collective-permute-start = (bf16[1,16,2048]{2,1,0:T(8,128)(2,1)}, bf16[1,16,2048]{2,1,0:T(8,128)(2,1)S(1)}, u32[]{:S(2)}, u32[]{:S(2)}) collective-permute-start(bf16[1,16,2048]{2,1,0:T(8,128)(2,1)} %bitcast.16), channel_id=1, source_target_pairs={{0,8},{8,16},{16,24},{24,32},{32,40},{40,48},{48,56},{56,0},{1,9},... | collective-permute-start | bytes 196616 | tf_op jit(solution)/shard_map/ppermute | solution.py:257
  4.2 25.3 %collective-permute-start.1 = (bf16[1,16,2048]{2,1,0:T(8,128)(2,1)}, bf16[1,16,2048]{2,1,0:T(8,128)(2,1)S(1)}, u32[]{:S(2)}, u32[]{:S(2)}) collective-permute-start(bf16[1,16,2048]{2,1,0:T(8,128)(2,1)} %bitcast.17), channel_id=1, source_target_pairs={{0,56},{8,0},{16,8},{24,16},{32,24},{40,32},{48,40},{56,48},{1,57}... | collective-permute-start | bytes 196616 | tf_op jit(solution)/shard_map/ppermute | solution.py:257
  8.0 0.7 copy-start.5
  8.7 0.7 copy-start.6
  10.5 40.4 %all-to-all-start = ((bf16[128,8,128]{2,1,0:T(8,128)(2,1)}), bf16[128,8,128]{2,1,0:T(8,128)(2,1)S(1)}, u32[]{:S(2)}, u32[]{:S(2)}) async-start(bf16[128,8,128]{2,1,0:T(8,128)(2,1)} %deal.1), calls=%async_computation | async-start | bytes 524288 | tf_op jit(solution)/shard_map/all_to_all | solution.py:279
  29.1 0.8 copy-start.7
  29.9 20.9 %collective-permute-start.2 = (bf16[3,16,2048]{2,1,0:T(8,128)(2,1)S(1)}, bf16[3,16,2048]{2,1,0:T(8,128)(2,1)S(1)}, u32[]{:S(2)}, u32[]{:S(2)}) collective-permute-start(bf16[3,16,2048]{2,1,0:T(8,128)(2,1)S(1)} %pad_maximum_fusion), channel_id=1, source_target_pairs={{0,24},{8,32},{16,40},{24,48},{32,56},{40,0},{48,8},{56,16},{1,25}... | collective-permute-start | bytes 589832 | tf_op jit(solution)/shard_map/ppermute | solution.py:257
  35.0 21.0 %collective-permute-start.3 = (bf16[2,16,2048]{2,1,0:T(8,128)(2,1)S(1)}, bf16[2,16,2048]{2,1,0:T(8,128)(2,1)S(1)}, u32[]{:S(2)}, u32[]{:S(2)}) collective-permute-start(bf16[2,16,2048]{2,1,0:T(8,128)(2,1)S(1)} %pad_maximum_fusion.1), channel_id=1, source_target_pairs={{0,40},{8,48},{16,56},{24,0},{32,8},{40,16},{48,24},{56,32},{1,41}... | collective-permute-start | bytes 393224 | tf_op jit(solution)/shard_map/ppermute | solution.py:257
  52.0 18.0 %all-to-all-start.1 = ((bf16[4,128,8,128]{3,2,1,0:T(8,128)(2,1)}), bf16[4,128,8,128]{3,2,1,0:T(8,128)(2,1)S(1)}, u32[]{:S(2)}, u32[]{:S(2)}) async-start(bf16[4,128,8,128]{3,2,1,0:T(8,128)(2,1)} %broadcast_in_dim.21), calls=%async_computation.1 | async-start | bytes 2097152 | tf_op jit(solution)/shard_map/all_to_all | solution.py:281
  56.1 19.2 %collective-permute-start.4 = (bf16[8,16,2048]{2,1,0:T(8,128)(2,1)S(1)}, bf16[8,16,2048]{2,1,0:T(8,128)(2,1)S(1)}, u32[]{:S(2)}, u32[]{:S(2)}) collective-permute-start(bf16[8,16,2048]{2,1,0:T(8,128)(2,1)S(1)} %constant_dynamic-update-slice_fusion.own), channel_id=1, source_target_pairs={{0,4},{4,0},{1,5},{5,1},{2,6},{6,2},{3,7},{7,3},{8,12},{12,8},{9,1... | collective-permute-start | bytes 1572872 | tf_op jit(solution)/shard_map/ppermute | solution.py:288
  71.1 5.5 %collective-permute-start.5 = (bf16[128,16,128]{2,1,0:T(8,128)(2,1)S(1)}, bf16[128,16,128]{2,1,0:T(8,128)(2,1)S(1)}, u32[]{:S(2)}, u32[]{:S(2)}) collective-permute-start(bf16[128,16,128]{2,1,0:T(8,128)(2,1)S(1)} %get-tuple-element.8.own), channel_id=1, source_target_pairs={{0,4},{4,0},{1,5},{5,1},{2,6},{6,2},{3,7},{7,3},{8,12},{12,8},{9,1... | collective-permute-start | bytes 1572872 | tf_op jit(solution)/shard_map/ppermute | solution.py:298
  75.3 1.3 copy-start.1
  75.3 1.3 copy-start.3
  81.2 13.1 %copy-start.8 = (s32[1,1,4,32,1]{3,4,2,1,0:T(1,128)S(1)}, s32[1,1,4,32,1]{3,4,2,1,0:T(1,128)}, u32[]{:S(2)}) copy-start(s32[1,1,4,32,1]{3,4,2,1,0:T(1,128)} %param.17) | copy-start | bytes 1540
  81.2 42.8 %all-to-all-start.2 = ((bf16[128,32,128]{2,1,0:T(8,128)(2,1)}), bf16[128,32,128]{2,1,0:T(8,128)(2,1)S(1)}, u32[]{:S(2)}, u32[]{:S(2)}) async-start(bf16[128,32,128]{2,1,0:T(8,128)(2,1)} %whiten.1), calls=%async_computation.2 | async-start | bytes 2097152 | tf_op jit(solution)/shard_map/all_to_all | solution.py:342
  93.1 0.7 copy-start.9
  95.2 28.8 %copy-start.2 = (bf16[768,256]{1,0:T(8,128)(2,1)S(1)}, bf16[768,256]{1,0:T(8,128)(2,1)}, u32[]{:S(2)}) copy-start(bf16[768,256]{1,0:T(8,128)(2,1)} %constant.80.clone.table) | copy-start | bytes 1179652
  95.8 28.2 %copy-start.4 = (f32[2,16,1,128]{3,2,1,0:T(1,128)S(1)}, f32[2,16,1,128]{3,2,1,0:T(1,128)}, u32[]{:S(2)}) copy-start(f32[2,16,1,128]{3,2,1,0:T(1,128)} %constant.79.clone.turns) | copy-start | bytes 49156
  125.2 7.7 %all-to-all-start.3 = ((bf16[4,32,256]{2,1,0:T(8,128)(2,1)}), bf16[4,32,256]{2,1,0:T(8,128)(2,1)S(1)}, u32[]{:S(2)}, u32[]{:S(2)}) async-start(bf16[4,32,256]{2,1,0:T(8,128)(2,1)} %broadcast_in_dim.24), calls=%async_computation.3 | async-start | bytes 131072 | tf_op jit(solution)/shard_map/all_to_all | solution.py:355

commit v3 on v2

--- a/solution.py
+++ b/solution.py
@@ -180,6 +180,12 @@
     left[...] = jnp.concatenate(lefts, axis=1).astype(bf16)
 
 
+def join_kernel(far_up, middle, far_down, out):
+    out[0:3] = far_up[...]
+    out[3:6] = middle[...]
+    out[6:8] = far_down[...]
+
+
 def project_kernel(place, own, other, right, col_flip, out):
     factor = right[...].reshape(DM, BLOCK)
     for side, rows in enumerate((own, other)):
@@ -253,6 +259,10 @@
     return pltpu.with_memory_space_constraint(array, pltpu.VMEM)
 
 
+def far(array):
+    return pltpu.with_memory_space_constraint(array, pltpu.HBM)
+
+
 def shift_y(rows, step):
     return lax.ppermute(rows, "y", [(i, (i + step) % NY) for i in range(NY)])
 
@@ -275,7 +285,7 @@
         ],
         compiler_params=grant(8),
         name="deal",
-    )(right_inv, left_inv)
+    )(far(right_inv), far(left_inv))
     pieces = lax.all_to_all(pieces, ROW_AXES, 0, 0, tiled=True)
     pieces = jnp.broadcast_to(pieces[None], (NE,) + pieces.shape)
     pieces = lax.all_to_all(pieces, "e", 0, 0, tiled=True)
@@ -284,7 +294,14 @@
     mine = grads.reshape(1, GROUP_ROWS, DM)
     near_rows = jnp.concatenate([shift_y(mine, 1), mine, shift_y(mine, -1)])
     far_up, far_down = shift_y(near_rows, 3), shift_y(near_rows[:2], -3)
-    rows_own = jnp.concatenate([far_up, near_rows, far_down])
+    rows_own = pl.pallas_call(
+        join_kernel,
+        out_shape=pltpu.VMEM((NY, GROUP_ROWS, DM), bf16),
+        in_specs=[IN_VMEM] * 3,
+        out_specs=IN_VMEM,
+        compiler_params=grant(4),
+        name="join",
+    )(near(far_up), near(near_rows), near(far_down))
     rows_other = lax.ppermute(rows_own, "c", swap)
     factor_shape = pltpu.VMEM((ROWS, GROUP_ROWS, BLOCK), bf16)
     right_cols, left_own = pl.pallas_call(

time: 155 us -> 149 us (0.961)
  blocking collectives: 20.1 us -> 53.8 us
  starting transfers between devices: 60.1 us -> 38.2 us
  waiting for transfers between devices: 56.3 us -> 40.6 us
  local copies, waits for them, and re-layouts: 5.57 us -> 3.66 us
    all_to_all x0 -> x1, blocking collectives: none -> 33.4 us  [shards(): pieces = lax.all_to_all(pieces, ROW_AXES, 0, 0, tiled=True)]
    all_to_all x1 -> x0, starting transfers between devices: 17.6 us -> none  [shards(): pieces = lax.all_to_all(pieces, ROW_AXES, 0, 0, tiled=True)]
    all_to_all x1, waiting for transfers between devices: 10.8 us -> 0.01 us  [shards(): pieces = lax.all_to_all(pieces, 'e', 0, 0, tiled=True)]
    ppermute x4, waiting for transfers between devices: 12.6 us -> 7.26 us  [shift_y(): return lax.ppermute(rows, 'y', [(i, (i + step) % NY) for i in range(NY)])]
    all_to_all x1, starting transfers between devices: 11.8 us -> 7.18 us  [shards(): partial_rows = lax.all_to_all(partial_cols, ROW_AXES, 0, 0, tiled=True)]
    ppermute x1, starting transfers between devices: 3.12 us -> 5.99 us  [shards(): rows_other = lax.ppermute(rows_own, 'c', swap)]
    ppermute x1, starting transfers between devices: 3.98 us -> 1.92 us  [shards(): left_other = lax.ppermute(left_own, 'c', swap)]
    unnamed x25 -> x17, local copies, waits for them, and re-layouts: 3.09 us -> 1.2 us
  transfers between devices with their start and end apart: 10 -> 9, of which waited for: 5 -> 5; matrix products, arithmetic and copies ran while one was open for 3% -> 2% of each run, Pallas kernels for 2% -> 1%
where the time goes in v3:
time: 149 us; the launch traced here: 148 us
  blocking collectives  53.8 us (36%)
  waiting for transfers between devices  40.6 us (27%)
  starting transfers between devices  38.2 us (26%)
  Pallas kernels  8.32 us (6%)
  local copies, waits for them, and re-layouts  3.66 us (2%)
  other arithmetic  3.18 us (2%)
    all_to_all x1, blocking collectives, shards(): pieces = lax.all_to_all(pieces, ROW_AXES, 0, 0, tiled=True)  33.4 us
    all_to_all x1, waiting for transfers between devices, shards(): partial_rows = lax.all_to_all(partial_cols, ROW_AXES, 0, 0, tiled=True)  28.2 us
    all_to_all x1, blocking collectives, shards(): arrived = lax.all_to_all(outgoing, ROW_AXES, 0, 0, tiled=True)  20.4 us
    ppermute x4, starting transfers between devices, shift_y(): return lax.ppermute(rows, 'y', [(i, (i + step) % NY) for i in range(NY)])  14.8 us
    ppermute x4, waiting for transfers between devices, shift_y(): return lax.ppermute(rows, 'y', [(i, (i + step) % NY) for i in range(NY)])  7.26 us
    all_to_all x1, starting transfers between devices, shards(): partial_rows = lax.all_to_all(partial_cols, ROW_AXES, 0, 0, tiled=True)  7.18 us
    ppermute x1, starting transfers between devices, shards(): rows_other = lax.ppermute(rows_own, 'c', swap)  5.99 us
    pallas_call x1, Pallas kernels, shards(): pl.pallas_call(whiten_kernel, out_shape=pltpu.VMEM((ROWS, 2 * GROUP_ROWS,...  4.6 us
  transfers between devices with their start and end apart: 9, of which 5 were waited for; matrix products, arithmetic and copies ran while one was open for 2% of the time, Pallas kernels for 1%

profile of v3, /device:TPU:1, one launch (start us, length us, event | category | flops | bytes accessed | tf_op | source)
XLA Modules:
  0.0 148.2 jit_solution(9527415325578200305)
XLA Ops:
  0.0 0.0 copy-start
  0.0 1.1 deal.1
  1.1 33.4 %all_to_all.25 = bf16[128,8,128]{2,1,0:T(8,128)(2,1)S(1)} all-to-all(bf16[128,8,128]{2,1,0:T(8,128)(2,1)S(1)} %deal.1), channel_id=1, replica_groups=mesh['z'=8,'y'=8,'c'=2,'e'=4] {'z','y','c'}, dimensions={0} | all-to-all | bytes 524288 | tf_op jit(solution)/shard_map/all_to_all | solution.py:289
  34.5 1.1 broadcast_in_dim.21
  35.6 0.0 copy-start.5
  35.7 4.1 %all-to-all-start.1 = ((bf16[4,128,8,128]{3,2,1,0:T(8,128)(2,1)}), bf16[4,128,8,128]{3,2,1,0:T(8,128)(2,1)S(1)}, u32[]{:S(2)}, u32[]{:S(2)}) async-start(bf16[4,128,8,128]{3,2,1,0:T(8,128)(2,1)} %broadcast_in_dim.21), calls=%async_computation.1 | async-start | bytes 2097152 | tf_op jit(solution)/shard_map/all_to_all | solution.py:291
  39.8 0.0 copy-done.5
  39.8 2.5 %collective-permute-start = (bf16[1,16,2048]{2,1,0:T(8,128)(2,1)S(1)}, bf16[1,16,2048]{2,1,0:T(8,128)(2,1)S(1)}, u32[]{:S(2)}, u32[]{:S(2)}) collective-permute-start(bf16[1,16,2048]{2,1,0:T(8,128)(2,1)S(1)} %bitcast.16), channel_id=1, source_target_pairs={{0,8},{8,16},{16,24},{24,32},{32,40},{40,48},{48,56},{56,0},{1,9},... | collective-permute-start | bytes 196616 | tf_op jit(solution)/shard_map/ppermute | solution.py:267
  42.3 4.0 %collective-permute-start.1 = (bf16[1,16,2048]{2,1,0:T(8,128)(2,1)S(1)}, bf16[1,16,2048]{2,1,0:T(8,128)(2,1)S(1)}, u32[]{:S(2)}, u32[]{:S(2)}) collective-permute-start(bf16[1,16,2048]{2,1,0:T(8,128)(2,1)S(1)} %bitcast.17), channel_id=1, source_target_pairs={{0,56},{8,0},{16,8},{24,16},{32,24},{40,32},{48,40},{56,48},{1,57}... | collective-permute-start | bytes 196616 | tf_op jit(solution)/shard_map/ppermute | solution.py:267
  46.3 0.0 copy-done
  46.3 0.1 reshape.206
  46.4 0.0 collective-permute-done
  46.4 1.2 collective-permute-done.1
  47.6 4.4 %collective-permute-start.2 = (bf16[3,16,2048]{2,1,0:T(8,128)(2,1)S(1)}, bf16[3,16,2048]{2,1,0:T(8,128)(2,1)S(1)}, u32[]{:S(2)}, u32[]{:S(2)}) collective-permute-start(bf16[3,16,2048]{2,1,0:T(8,128)(2,1)S(1)} %pad_maximum_fusion.middle), channel_id=1, source_target_pairs={{0,24},{8,32},{16,40},{24,48},{32,56},{40,0},{48,8},{56,16},{1,25}... | collective-permute-start | bytes 589832 | tf_op jit(solution)/shard_map/ppermute | solution.py:267
  52.0 3.9 %collective-permute-start.3 = (bf16[2,16,2048]{2,1,0:T(8,128)(2,1)S(1)}, bf16[2,16,2048]{2,1,0:T(8,128)(2,1)S(1)}, u32[]{:S(2)}, u32[]{:S(2)}) collective-permute-start(bf16[2,16,2048]{2,1,0:T(8,128)(2,1)S(1)} %pad_maximum_fusion.1), channel_id=1, source_target_pairs={{0,40},{8,48},{16,56},{24,0},{32,8},{40,16},{48,24},{56,32},{1,41}... | collective-permute-start | bytes 393224 | tf_op jit(solution)/shard_map/ppermute | solution.py:267
  56.0 0.8 convert_bitcast_fusion
  56.7 0.4 copy.21.row_flip
  57.1 6.1 %collective-permute-done.3.far_down = bf16[2,16,2048]{2,1,0:T(8,128)(2,1)S(1)} collective-permute-done((bf16[2,16,2048]{2,1,0:T(8,128)(2,1)S(1)}, bf16[2,16,2048]{2,1,0:T(8,128)(2,1)S(1)}, u32[]{:S(2)}, u32[]{:S(2)}) %collective-permute-start.3) | collective-permute-done | bytes 131104 | tf_op jit(solution)/shard_map/ppermute | solution.py:267
  63.2 0.0 collective-permute-done.2.far_up
  63.3 6.0 %collective-permute-start.4 = (bf16[8,16,2048]{2,1,0:T(8,128)(2,1)S(1)}, bf16[8,16,2048]{2,1,0:T(8,128)(2,1)S(1)}, u32[]{:S(2)}, u32[]{:S(2)}) collective-permute-start(bf16[8,16,2048]{2,1,0:T(8,128)(2,1)S(1)} %join.1.own), channel_id=1, source_target_pairs={{0,4},{4,0},{1,5},{5,1},{2,6},{6,2},{3,7},{7,3},{8,12},{12,8},{9,1... | collective-permute-start | bytes 1572872 | tf_op jit(solution)/shard_map/ppermute | solution.py:305
  69.3 0.0 all-to-all-done.1.pieces
  69.3 1.1 arrange.1
  70.4 1.9 %collective-permute-start.5 = (bf16[128,16,128]{2,1,0:T(8,128)(2,1)S(1)}, bf16[128,16,128]{2,1,0:T(8,128)(2,1)S(1)}, u32[]{:S(2)}, u32[]{:S(2)}) collective-permute-start(bf16[128,16,128]{2,1,0:T(8,128)(2,1)S(1)} %get-tuple-element.8.own), channel_id=1, source_target_pairs={{0,4},{4,0},{1,5},{5,1},{2,6},{6,2},{3,7},{7,3},{8,12},{12,8},{9,1... | collective-permute-start | bytes 1572872 | tf_op jit(solution)/shard_map/ppermute | solution.py:315
  72.3 0.1 pad_add_fusion.place
  72.4 0.1 select_reduce_fusion
  72.5 0.0 collective-permute-done.4.other
  72.5 0.0 copy-start.1
  72.5 0.0 copy-start.3
  72.6 1.0 project.1.tile
  73.5 0.7 collective-permute-done.5.other
  74.2 0.0 copy-done.1
  74.2 0.0 copy-done.3
  74.2 4.6 %whiten.1 = bf16[128,32,128]{2,1,0:T(8,128)(2,1)} custom-call(s32[2]{0:T(128)S(1)} %pad_add_fusion.place, bf16[256,128]{1,0:T(8,128)(2,1)S(1)} %project.1.tile, bf16[128,16,128]{2,1,0:T(8,128)(2,1)S(1)} %get-tuple-element.8.own, bf16[128,16,128]{2,1,0:T(8,128)(2,1)S(1)} %collective-permute-done.5.other, f32[2048,1]{1,0:T(8,128)S(1)} %copy.21.row_flip, ...), custom_call_target="tpu_custom_call" | custom-call | tf_op jit(solution)/shard_map/whiten/pallas_call | solution.py:347
  78.8 0.0 copy-start.6
  78.8 7.2 %all-to-all-start.2 = ((bf16[128,32,128]{2,1,0:T(8,128)(2,1)}), bf16[128,32,128]{2,1,0:T(8,128)(2,1)S(1)}, u32[]{:S(2)}, u32[]{:S(2)}) async-start(bf16[128,32,128]{2,1,0:T(8,128)(2,1)} %whiten.1), calls=%async_computation.2 | async-start | bytes 2097152 | tf_op jit(solution)/shard_map/all_to_all | solution.py:359
  86.0 0.0 copy-start.7
  86.0 0.6 copy-done.7
  86.7 0.1 copy.22
  86.7 0.5 broadcast.215
  87.3 0.0 copy-done.6
  87.3 0.7 reduce.7
  87.9 0.1 reshape_squeeze.3
  88.0 0.1 convert_reduce_fusion
  88.1 0.0 copy-start.2
  88.1 0.5 fusion
  88.7 0.0 copy-start.4
  88.8 28.2 %all-to-all-done.2.parts = bf16[128,32,128]{2,1,0:T(8,128)(2,1)S(1)} async-done(((bf16[128,32,128]{2,1,0:T(8,128)(2,1)}), bf16[128,32,128]{2,1,0:T(8,128)(2,1)S(1)}, u32[]{:S(2)}, u32[]{:S(2)}) %all-to-all-start.2) | async-done | bytes 1048608 | tf_op jit(solution)/shard_map/all_to_all | solution.py:359
  117.0 0.0 copy-done.2
  117.0 0.0 copy-done.4
  117.0 0.5 spectrum.1
  117.5 0.6 broadcast_in_dim.24
  118.1 4.2 %all-to-all-start.3 = ((bf16[4,32,256]{2,1,0:T(8,128)(2,1)}), bf16[4,32,256]{2,1,0:T(8,128)(2,1)S(1)}, u32[]{:S(2)}, u32[]{:S(2)}) async-start(bf16[4,32,256]{2,1,0:T(8,128)(2,1)} %broadcast_in_dim.24), calls=%async_computation.3 | async-start | bytes 131072 | tf_op jit(solution)/shard_map/all_to_all | solution.py:372
  122.4 4.5 %all-to-all-done.3 = bf16[4,32,256]{2,1,0:T(8,128)(2,1)S(1)} async-done(((bf16[4,32,256]{2,1,0:T(8,128)(2,1)}), bf16[4,32,256]{2,1,0:T(8,128)(2,1)S(1)}, u32[]{:S(2)}, u32[]{:S(2)}) %all-to-all-start.3) | async-done | bytes 65568 | tf_op jit(solution)/shard_map/all_to_all | solution.py:372
  126.8 0.2 convolution_convert_fusion
  127.0 0.1 reshape.208
  127.1 20.4 %all_to_all.26 = bf16[128,2,256]{2,1,0:T(2,128)(2,1)S(1)} all-to-all(bf16[128,2,256]{2,1,0:T(2,128)(2,1)S(1)} %reshape.208), channel_id=1, replica_groups=mesh['z'=8,'y'=8,'c'=2,'e'=4] {'z','y','c'}, dimensions={0} | all-to-all | bytes 262144 | tf_op jit(solution)/shard_map/all_to_all | solution.py:378
  147.4 0.8 bitcast_convert_fusion
  (13 shorter events, 0.2 us)
Async XLA Ops:
  0.0 46.3 %copy-start = (s32[1,4,2048]{2,1,0:T(4,128)S(1)}, s32[1,4,2048]{2,1,0:T(4,128)}, u32[]{:S(2)}) copy-start(s32[1,4,2048]{2,1,0:T(4,128)} %param.15) | copy-start | bytes 98308
  35.6 4.1 %copy-start.5 = (bf16[1,1,16,2048]{3,2,1,0:T(8,128)(2,1)S(1)}, bf16[1,1,16,2048]{3,2,1,0:T(8,128)(2,1)}, u32[]{:S(2)}) copy-start(bf16[1,1,16,2048]{3,2,1,0:T(8,128)(2,1)} %param.11) | copy-start | bytes 196612
  35.7 33.6 %all-to-all-start.1 = ((bf16[4,128,8,128]{3,2,1,0:T(8,128)(2,1)}), bf16[4,128,8,128]{3,2,1,0:T(8,128)(2,1)S(1)}, u32[]{:S(2)}, u32[]{:S(2)}) async-start(bf16[4,128,8,128]{3,2,1,0:T(8,128)(2,1)} %broadcast_in_dim.21), calls=%async_computation.1 | async-start | bytes 2097152 | tf_op jit(solution)/shard_map/all_to_all | solution.py:291
  39.8 6.6 %collective-permute-start = (bf16[1,16,2048]{2,1,0:T(8,128)(2,1)S(1)}, bf16[1,16,2048]{2,1,0:T(8,128)(2,1)S(1)}, u32[]{:S(2)}, u32[]{:S(2)}) collective-permute-start(bf16[1,16,2048]{2,1,0:T(8,128)(2,1)S(1)} %bitcast.16), channel_id=1, source_target_pairs={{0,8},{8,16},{16,24},{24,32},{32,40},{40,48},{48,56},{56,0},{1,9},... | collective-permute-start | bytes 196616 | tf_op jit(solution)/shard_map/ppermute | solution.py:267
  42.3 5.3 %collective-permute-start.1 = (bf16[1,16,2048]{2,1,0:T(8,128)(2,1)S(1)}, bf16[1,16,2048]{2,1,0:T(8,128)(2,1)S(1)}, u32[]{:S(2)}, u32[]{:S(2)}) collective-permute-start(bf16[1,16,2048]{2,1,0:T(8,128)(2,1)S(1)} %bitcast.17), channel_id=1, source_target_pairs={{0,56},{8,0},{16,8},{24,16},{32,24},{40,32},{48,40},{56,48},{1,57}... | collective-permute-start | bytes 196616 | tf_op jit(solution)/shard_map/ppermute | solution.py:267
  47.6 15.6 %collective-permute-start.2 = (bf16[3,16,2048]{2,1,0:T(8,128)(2,1)S(1)}, bf16[3,16,2048]{2,1,0:T(8,128)(2,1)S(1)}, u32[]{:S(2)}, u32[]{:S(2)}) collective-permute-start(bf16[3,16,2048]{2,1,0:T(8,128)(2,1)S(1)} %pad_maximum_fusion.middle), channel_id=1, source_target_pairs={{0,24},{8,32},{16,40},{24,48},{32,56},{40,0},{48,8},{56,16},{1,25}... | collective-permute-start | bytes 589832 | tf_op jit(solution)/shard_map/ppermute | solution.py:267
  52.0 11.2 %collective-permute-start.3 = (bf16[2,16,2048]{2,1,0:T(8,128)(2,1)S(1)}, bf16[2,16,2048]{2,1,0:T(8,128)(2,1)S(1)}, u32[]{:S(2)}, u32[]{:S(2)}) collective-permute-start(bf16[2,16,2048]{2,1,0:T(8,128)(2,1)S(1)} %pad_maximum_fusion.1), channel_id=1, source_target_pairs={{0,40},{8,48},{16,56},{24,0},{32,8},{40,16},{48,24},{56,32},{1,41}... | collective-permute-start | bytes 393224 | tf_op jit(solution)/shard_map/ppermute | solution.py:267
  63.3 9.3 %collective-permute-start.4 = (bf16[8,16,2048]{2,1,0:T(8,128)(2,1)S(1)}, bf16[8,16,2048]{2,1,0:T(8,128)(2,1)S(1)}, u32[]{:S(2)}, u32[]{:S(2)}) collective-permute-start(bf16[8,16,2048]{2,1,0:T(8,128)(2,1)S(1)} %join.1.own), channel_id=1, source_target_pairs={{0,4},{4,0},{1,5},{5,1},{2,6},{6,2},{3,7},{7,3},{8,12},{12,8},{9,1... | collective-permute-start | bytes 1572872 | tf_op jit(solution)/shard_map/ppermute | solution.py:305
  70.4 3.8 %collective-permute-start.5 = (bf16[128,16,128]{2,1,0:T(8,128)(2,1)S(1)}, bf16[128,16,128]{2,1,0:T(8,128)(2,1)S(1)}, u32[]{:S(2)}, u32[]{:S(2)}) collective-permute-start(bf16[128,16,128]{2,1,0:T(8,128)(2,1)S(1)} %get-tuple-element.8.own), channel_id=1, source_target_pairs={{0,4},{4,0},{1,5},{5,1},{2,6},{6,2},{3,7},{7,3},{8,12},{12,8},{9,1... | collective-permute-start | bytes 1572872 | tf_op jit(solution)/shard_map/ppermute | solution.py:315
  72.5 1.7 %copy-start.1 = (bf16[512,768]{1,0:T(8,128)(2,1)S(1)}, bf16[512,768]{1,0:T(8,128)(2,1)}, u32[]{:S(2)}) copy-start(bf16[512,768]{1,0:T(8,128)(2,1)} %constant.77.clone.table) | copy-start | bytes 2359300
  72.5 1.6 %copy-start.3 = (f32[256,16]{1,0:T(8,128)S(1)}, f32[256,16]{1,0:T(8,128)}, u32[]{:S(2)}) copy-start(f32[256,16]{1,0:T(8,128)} %constant.78.clone.twiddles) | copy-start | bytes 49156
  78.8 8.5 %copy-start.6 = (s32[1,1,4,32,1]{3,4,2,1,0:T(1,128)S(1)}, s32[1,1,4,32,1]{3,4,2,1,0:T(1,128)}, u32[]{:S(2)}) copy-start(s32[1,1,4,32,1]{3,4,2,1,0:T(1,128)} %param.17) | copy-start | bytes 1540
  78.8 38.2 %all-to-all-start.2 = ((bf16[128,32,128]{2,1,0:T(8,128)(2,1)}), bf16[128,32,128]{2,1,0:T(8,128)(2,1)S(1)}, u32[]{:S(2)}, u32[]{:S(2)}) async-start(bf16[128,32,128]{2,1,0:T(8,128)(2,1)} %whiten.1), calls=%async_computation.2 | async-start | bytes 2097152 | tf_op jit(solution)/shard_map/all_to_all | solution.py:359
  86.0 0.7 copy-start.7
  88.1 28.8 %copy-start.2 = (bf16[768,256]{1,0:T(8,128)(2,1)S(1)}, bf16[768,256]{1,0:T(8,128)(2,1)}, u32[]{:S(2)}) copy-start(bf16[768,256]{1,0:T(8,128)(2,1)} %constant.80.clone.table) | copy-start | bytes 1179652
  88.7 28.2 %copy-start.4 = (f32[2,16,1,128]{3,2,1,0:T(1,128)S(1)}, f32[2,16,1,128]{3,2,1,0:T(1,128)}, u32[]{:S(2)}) copy-start(f32[2,16,1,128]{3,2,1,0:T(1,128)} %constant.79.clone.turns) | copy-start | bytes 49156
  118.1 8.7 %all-to-all-start.3 = ((bf16[4,32,256]{2,1,0:T(8,128)(2,1)}), bf16[4,32,256]{2,1,0:T(8,128)(2,1)S(1)}, u32[]{:S(2)}, u32[]{:S(2)}) async-start(bf16[4,32,256]{2,1,0:T(8,128)(2,1)} %broadcast_in_dim.24), calls=%async_computation.3 | async-start | bytes 131072 | tf_op jit(solution)/shard_map/all_to_all | solution.py:372

commit v4 on v2

--- a/solution.py
+++ b/solution.py
@@ -156,7 +156,9 @@
                 out[z * NYC + yc] = both.astype(bf16)
 
 
-def arrange_kernel(pieces, right, left):
+def arrange_kernel(place, own, first_shared, second_shared, third_shared, right, left, pieces):
+    for step, piece in enumerate((own, first_shared, second_shared, third_shared)):
+        pieces[(place[0] + NE - step) % NE] = piece[...]
     quarter = GROUP_ROWS // NE
     pack = BLOCK // NE
     shape = (ROWS, 2 * quarter, BLOCK)
@@ -186,9 +188,8 @@
         part = dot(rows[...].reshape(TILE_ROWS // NC, DM), factor) * col_flip[...]
         part = part.astype(bf16).reshape(NY, GROUP_ROWS, BLOCK)
         for k in range(NY):
-            from_y = (place[0] + NY // 2 + k) % NY
             from_c = place[1] if side == 0 else 1 - place[1]
-            start = pl.multiple_of(GROUP_ROWS * (NC * from_y + from_c), GROUP_ROWS)
+            start = pl.multiple_of(GROUP_ROWS * (NC * k + from_c), GROUP_ROWS)
             out[pl.ds(start, GROUP_ROWS), :] = part[k]
 
 
@@ -253,8 +254,8 @@
     return pltpu.with_memory_space_constraint(array, pltpu.VMEM)
 
 
-def shift_y(rows, step):
-    return lax.ppermute(rows, "y", [(i, (i + step) % NY) for i in range(NY)])
+def far(array):
+    return pltpu.with_memory_space_constraint(array, pltpu.HBM)
 
 
 def shards(grads, right_inv, left_inv, row_signs, col_signs, listed, owners):
@@ -275,29 +276,28 @@
         ],
         compiler_params=grant(8),
         name="deal",
-    )(right_inv, left_inv)
+    )(far(right_inv), far(left_inv))
     pieces = lax.all_to_all(pieces, ROW_AXES, 0, 0, tiled=True)
-    pieces = jnp.broadcast_to(pieces[None], (NE,) + pieces.shape)
-    pieces = lax.all_to_all(pieces, "e", 0, 0, tiled=True)
-
+    shared = [
+        lax.ppermute(pieces, "e", [(i, (i + step) % NE) for i in range(NE)])
+        for step in range(1, NE)
+    ]
+    rows_own = jnp.broadcast_to(grads.reshape(1, GROUP_ROWS, DM), (NY, GROUP_ROWS, DM))
+    rows_own = lax.all_to_all(rows_own, "y", 0, 0, tiled=True)
     swap = [(0, 1), (1, 0)]
-    mine = grads.reshape(1, GROUP_ROWS, DM)
-    near_rows = jnp.concatenate([shift_y(mine, 1), mine, shift_y(mine, -1)])
-    far_up, far_down = shift_y(near_rows, 3), shift_y(near_rows[:2], -3)
-    rows_own = jnp.concatenate([far_up, near_rows, far_down])
     rows_other = lax.ppermute(rows_own, "c", swap)
+    place = jnp.stack([e_id, c_id])
     factor_shape = pltpu.VMEM((ROWS, GROUP_ROWS, BLOCK), bf16)
     right_cols, left_own = pl.pallas_call(
         arrange_kernel,
         out_shape=(factor_shape, factor_shape),
-        in_specs=[IN_VMEM],
+        in_specs=[IN_SMEM] + [IN_VMEM] * NE,
         out_specs=(IN_VMEM, IN_VMEM),
+        scratch_shapes=[pltpu.VMEM((NE, ROWS, 2 * GROUP_ROWS // NE, BLOCK), bf16)],
         compiler_params=grant(12),
         name="arrange",
-    )(near(pieces))
+    )(place, *[near(piece) for piece in [pieces] + shared])
     left_other = lax.ppermute(left_own, "c", swap)
-    place = jnp.stack([y_id, c_id])
-
     row_bits = lax.dynamic_index_in_dim(row_signs[0], e_id, 0, keepdims=False)
     row_flip = (1 - 2 * row_bits).astype(f32)[:, None]
     col_bits = lax.dynamic_index_in_dim(col_signs[0], e_id, 0, keepdims=False)

time: 155 us -> 145 us (0.935)
  blocking collectives: 20.1 us -> 53.9 us
  starting transfers between devices: 60.1 us -> 32.9 us
  waiting for transfers between devices: 56.3 us -> 41 us
  local copies, waits for them, and re-layouts: 5.57 us -> 3.4 us
    all_to_all x0 -> x1, blocking collectives: none -> 33.6 us  [shards(): pieces = lax.all_to_all(pieces, ROW_AXES, 0, 0, tiled=True)]
    all_to_all x2 -> x1, starting transfers between devices: 21.7 us -> 3.49 us  [shards(): rows_own = lax.all_to_all(rows_own, 'y', 0, 0, tiled=True)]
    all_to_all x2 -> x1, waiting for transfers between devices: 10.8 us -> 0.01 us  [shards(): rows_own = lax.all_to_all(rows_own, 'y', 0, 0, tiled=True)]
    ppermute x4 -> x3, starting transfers between devices: 16.3 us -> 10.5 us  [shards(): lax.ppermute(pieces, 'e', [(i, (i + step) % NE) for i in range(NE)])]
    ppermute x4 -> x3, waiting for transfers between devices: 12.6 us -> 7.78 us  [shards(): lax.ppermute(pieces, 'e', [(i, (i + step) % NE) for i in range(NE)])]
    all_to_all x1, starting transfers between devices: 11.8 us -> 9.46 us  [shards(): partial_rows = lax.all_to_all(partial_cols, ROW_AXES, 0, 0, tiled=True)]
    unnamed x25 -> x17, local copies, waits for them, and re-layouts: 3.09 us -> 1.2 us
  transfers between devices with their start and end apart: 10 -> 8, of which waited for: 5 -> 5; matrix products, arithmetic and copies ran while one was open for 3% -> 2% of each run, Pallas kernels for 2% -> 2%
where the time goes in v4:
time: 145 us; the launch traced here: 144 us
  blocking collectives  53.9 us (37%)
  waiting for transfers between devices  41 us (28%)
  starting transfers between devices  32.9 us (23%)
  Pallas kernels  9.47 us (7%)
  local copies, waits for them, and re-layouts  3.4 us (2%)
  other arithmetic  3.14 us (2%)
    all_to_all x1, blocking collectives, shards(): pieces = lax.all_to_all(pieces, ROW_AXES, 0, 0, tiled=True)  33.6 us
    all_to_all x1, waiting for transfers between devices, shards(): partial_rows = lax.all_to_all(partial_cols, ROW_AXES, 0, 0, tiled=True)  28.2 us
    all_to_all x1, blocking collectives, shards(): arrived = lax.all_to_all(outgoing, ROW_AXES, 0, 0, tiled=True)  20.4 us
    ppermute x3, starting transfers between devices, shards(): lax.ppermute(pieces, 'e', [(i, (i + step) % NE) for i in range(NE)])  10.5 us
    all_to_all x1, starting transfers between devices, shards(): partial_rows = lax.all_to_all(partial_cols, ROW_AXES, 0, 0, tiled=True)  9.46 us
    ppermute x3, waiting for transfers between devices, shards(): lax.ppermute(pieces, 'e', [(i, (i + step) % NE) for i in range(NE)])  7.78 us
    pallas_call x1, Pallas kernels, shards(): pl.pallas_call(whiten_kernel, out_shape=pltpu.VMEM((ROWS, 2 * GROUP_ROWS,...  4.6 us
    all_to_all x1, waiting for transfers between devices, shards(): lax.all_to_all(jnp.broadcast_to(picked[None], (NE,) + picked.shape), 'e',...  4.47 us
  transfers between devices with their start and end apart: 8, of which 5 were waited for; matrix products, arithmetic and copies ran while one was open for 2% of the time, Pallas kernels for 2%

profile of v4, /device:TPU:1, one launch (start us, length us, event | category | flops | bytes accessed | tf_op | source)
XLA Modules:
  0.0 144.3 jit_solution(12293987369971466734)
XLA Ops:
  0.0 0.0 copy-start
  0.0 1.1 deal.1
  1.1 0.0 copy-start.5
  1.1 33.6 %all_to_all.25.own = bf16[128,8,128]{2,1,0:T(8,128)(2,1)S(1)} all-to-all(bf16[128,8,128]{2,1,0:T(8,128)(2,1)S(1)} %deal.1), channel_id=1, replica_groups=mesh['z'=8,'y'=8,'c'=2,'e'=4] {'z','y','c'}, dimensions={0} | all-to-all | bytes 524288 | tf_op jit(solution)/shard_map/all_to_all | solution.py:280
  34.7 0.0 copy-done.5
  34.7 0.8 broadcast_in_dim.24
  35.5 3.5 %all-to-all-start = ((bf16[8,16,2048]{2,1,0:T(8,128)(2,1)}), bf16[8,16,2048]{2,1,0:T(8,128)(2,1)S(1)}, u32[]{:S(2)}, u32[]{:S(2)}) async-start(bf16[8,16,2048]{2,1,0:T(8,128)(2,1)} %broadcast_in_dim.24), calls=%async_computation | async-start | bytes 1048576 | tf_op jit(solution)/shard_map/all_to_all | solution.py:286
  39.0 3.1 %collective-permute-start.1 = (bf16[128,8,128]{2,1,0:T(8,128)(2,1)S(1)}, bf16[128,8,128]{2,1,0:T(8,128)(2,1)S(1)}, u32[]{:S(2)}, u32[]{:S(2)}) collective-permute-start(bf16[128,8,128]{2,1,0:T(8,128)(2,1)S(1)} %all_to_all.25.own), channel_id=1, source_target_pairs={{0,1},{1,2},{2,3},{3,0},{4,5},{5,6},{6,7},{7,4},{8,9},{9,10},{10,1... | collective-permute-start | bytes 786440 | tf_op jit(solution)/shard_map/ppermute | solution.py:282
  42.2 4.4 %collective-permute-start.2 = (bf16[128,8,128]{2,1,0:T(8,128)(2,1)S(1)}, bf16[128,8,128]{2,1,0:T(8,128)(2,1)S(1)}, u32[]{:S(2)}, u32[]{:S(2)}) collective-permute-start(bf16[128,8,128]{2,1,0:T(8,128)(2,1)S(1)} %all_to_all.25.own), channel_id=1, source_target_pairs={{0,2},{1,3},{2,0},{3,1},{4,6},{5,7},{6,4},{7,5},{8,10},{9,11},{10,... | collective-permute-start | bytes 786440 | tf_op jit(solution)/shard_map/ppermute | solution.py:282
  46.5 3.1 %collective-permute-start.3 = (bf16[128,8,128]{2,1,0:T(8,128)(2,1)S(1)}, bf16[128,8,128]{2,1,0:T(8,128)(2,1)S(1)}, u32[]{:S(2)}, u32[]{:S(2)}) collective-permute-start(bf16[128,8,128]{2,1,0:T(8,128)(2,1)S(1)} %all_to_all.25.own), channel_id=1, source_target_pairs={{0,3},{1,0},{2,1},{3,2},{4,7},{5,4},{6,5},{7,6},{8,11},{9,8},{10,9... | collective-permute-start | bytes 786440 | tf_op jit(solution)/shard_map/ppermute | solution.py:282
  49.6 0.1 pad_add_fusion.place
  49.7 0.0 collective-permute-done.1.first_shared
  49.7 6.5 %collective-permute-done.2.second_shared = bf16[128,8,128]{2,1,0:T(8,128)(2,1)S(1)} collective-permute-done((bf16[128,8,128]{2,1,0:T(8,128)(2,1)S(1)}, bf16[128,8,128]{2,1,0:T(8,128)(2,1)S(1)}, u32[]{:S(2)}, u32[]{:S(2)}) %collective-permute-start.2) | collective-permute-done | bytes 262176 | tf_op jit(solution)/shard_map/ppermute | solution.py:282
  56.2 1.2 collective-permute-done.3.third_shared
  57.5 1.7 %arrange.1 = (bf16[128,16,128]{2,1,0:T(8,128)(2,1)S(1)}, bf16[128,16,128]{2,1,0:T(8,128)(2,1)S(1)}) custom-call(s32[2]{0:T(128)S(1)} %pad_add_fusion.place, bf16[128,8,128]{2,1,0:T(8,128)(2,1)S(1)} %all_to_all.25.own, bf16[128,8,128]{2,1,0:T(8,128)(2,1)S(1)} %collective-permute-done.1.first_shared, ...), custom_call_target="tpu_custom_call" | custom-call | tf_op jit(solution)/shard_map/arrange/pallas_call | solution.py:291
  59.2 3.4 %collective-permute-start.4 = (bf16[128,16,128]{2,1,0:T(8,128)(2,1)S(1)}, bf16[128,16,128]{2,1,0:T(8,128)(2,1)S(1)}, u32[]{:S(2)}, u32[]{:S(2)}) collective-permute-start(bf16[128,16,128]{2,1,0:T(8,128)(2,1)S(1)} %get-tuple-element.8.own), channel_id=1, source_target_pairs={{0,4},{4,0},{1,5},{5,1},{2,6},{6,2},{3,7},{7,3},{8,12},{12,8},{9,1... | collective-permute-start | bytes 1572872 | tf_op jit(solution)/shard_map/ppermute | solution.py:300
  62.6 0.0 all-to-all-done.own
  62.6 1.9 %collective-permute-start = (bf16[8,16,2048]{2,1,0:T(8,128)(2,1)S(1)}, bf16[8,16,2048]{2,1,0:T(8,128)(2,1)}, u32[]{:S(2)}, u32[]{:S(2)}) collective-permute-start(bf16[8,16,2048]{2,1,0:T(8,128)(2,1)S(1)} %all-to-all-done.own), channel_id=1, source_target_pairs={{0,4},{4,0},{1,5},{5,1},{2,6},{6,2},{3,7},{7,3},{8,12},{12,8},{9,1... | collective-permute-start | bytes 1572872 | tf_op jit(solution)/shard_map/ppermute | solution.py:288
  64.5 0.8 convert_bitcast_fusion
  65.3 0.0 copy-done
  65.4 0.1 reshape.203
  65.5 0.4 copy.21.row_flip
  65.9 0.1 select_reduce_fusion
  66.0 0.6 collective-permute-done.other
  66.6 0.0 copy-start.1
  66.6 0.0 copy-start.3
  66.6 1.6 %project.1.tile = bf16[256,128]{1,0:T(8,128)(2,1)S(1)} custom-call(s32[2]{0:T(128)S(1)} %pad_add_fusion.place, bf16[8,16,2048]{2,1,0:T(8,128)(2,1)S(1)} %all-to-all-done.own, bf16[8,16,2048]{2,1,0:T(8,128)(2,1)} %collective-permute-done.other, bf16[128,16,128]{2,1,0:T(8,128)(2,1)S(1)} %get-tuple-element.7.right, f32[1,128]{1,0:T(1,128)S(1)} %convert_bitcast_fusion.1.col_flip), custom_call_target="tpu_custom_call" | custom-call | tf_op jit(solution)/shard_map/project/pallas_call | solution.py:322
  68.1 0.0 collective-permute-done.4.other
  68.1 0.0 copy-done.1
  68.1 0.0 copy-done.3
  68.1 4.6 %whiten.1 = bf16[128,32,128]{2,1,0:T(8,128)(2,1)} custom-call(s32[2]{0:T(128)S(1)} %pad_add_fusion.place, bf16[256,128]{1,0:T(8,128)(2,1)S(1)} %project.1.tile, bf16[128,16,128]{2,1,0:T(8,128)(2,1)S(1)} %get-tuple-element.8.own, bf16[128,16,128]{2,1,0:T(8,128)(2,1)S(1)} %collective-permute-done.4.other, f32[2048,1]{1,0:T(8,128)S(1)} %copy.21.row_flip, ...), custom_call_target="tpu_custom_call" | custom-call | tf_op jit(solution)/shard_map/whiten/pallas_call | solution.py:330
  72.7 0.0 copy-start.6
  72.7 9.5 %all-to-all-start.2 = ((bf16[128,32,128]{2,1,0:T(8,128)(2,1)}), bf16[128,32,128]{2,1,0:T(8,128)(2,1)S(1)}, u32[]{:S(2)}, u32[]{:S(2)}) async-start(bf16[128,32,128]{2,1,0:T(8,128)(2,1)} %whiten.1), calls=%async_computation.2 | async-start | bytes 2097152 | tf_op jit(solution)/shard_map/all_to_all | solution.py:342
  82.2 0.0 copy-start.7
  82.2 0.6 copy-done.7
  82.9 0.1 copy.22
  83.0 0.5 broadcast.214
  83.5 0.0 copy-done.6
  83.5 0.7 reduce.7
  84.1 0.1 reshape_squeeze.3
  84.2 0.1 convert_reduce_fusion
  84.4 0.0 copy-start.2
  84.4 0.5 fusion
  84.9 0.0 copy-start.4
  85.0 28.2 %all-to-all-done.2.parts = bf16[128,32,128]{2,1,0:T(8,128)(2,1)S(1)} async-done(((bf16[128,32,128]{2,1,0:T(8,128)(2,1)}), bf16[128,32,128]{2,1,0:T(8,128)(2,1)S(1)}, u32[]{:S(2)}, u32[]{:S(2)}) %all-to-all-start.2) | async-done | bytes 1048608 | tf_op jit(solution)/shard_map/all_to_all | solution.py:342
  113.2 0.0 copy-done.2
  113.2 0.0 copy-done.4
  113.2 0.5 spectrum.1
  113.7 0.6 broadcast_in_dim.46
  114.4 4.0 %all-to-all-start.3 = ((bf16[4,32,256]{2,1,0:T(8,128)(2,1)}), bf16[4,32,256]{2,1,0:T(8,128)(2,1)S(1)}, u32[]{:S(2)}, u32[]{:S(2)}) async-start(bf16[4,32,256]{2,1,0:T(8,128)(2,1)} %broadcast_in_dim.46), calls=%async_computation.3 | async-start | bytes 131072 | tf_op jit(solution)/shard_map/all_to_all | solution.py:355
  118.4 4.5 %all-to-all-done.3 = bf16[4,32,256]{2,1,0:T(8,128)(2,1)S(1)} async-done(((bf16[4,32,256]{2,1,0:T(8,128)(2,1)}), bf16[4,32,256]{2,1,0:T(8,128)(2,1)S(1)}, u32[]{:S(2)}, u32[]{:S(2)}) %all-to-all-start.3) | async-done | bytes 65568 | tf_op jit(solution)/shard_map/all_to_all | solution.py:355
  122.9 0.2 convolution_convert_fusion
  123.1 0.1 reshape.205
  123.1 20.4 %all_to_all.26 = bf16[128,2,256]{2,1,0:T(2,128)(2,1)S(1)} all-to-all(bf16[128,2,256]{2,1,0:T(2,128)(2,1)S(1)} %reshape.205), channel_id=1, replica_groups=mesh['z'=8,'y'=8,'c'=2,'e'=4] {'z','y','c'}, dimensions={0} | all-to-all | bytes 262144 | tf_op jit(solution)/shard_map/all_to_all | solution.py:361
  143.5 0.8 bitcast_convert_fusion
  (10 shorter events, 0.1 us)
Async XLA Ops:
  0.0 65.3 %copy-start = (s32[1,4,2048]{2,1,0:T(4,128)S(1)}, s32[1,4,2048]{2,1,0:T(4,128)}, u32[]{:S(2)}) copy-start(s32[1,4,2048]{2,1,0:T(4,128)} %param.15) | copy-start | bytes 98308
  1.1 33.6 %copy-start.5 = (bf16[1,1,16,2048]{3,2,1,0:T(8,128)(2,1)S(1)}, bf16[1,1,16,2048]{3,2,1,0:T(8,128)(2,1)}, u32[]{:S(2)}) copy-start(bf16[1,1,16,2048]{3,2,1,0:T(8,128)(2,1)} %param.11) | copy-start | bytes 196612
  35.5 27.1 %all-to-all-start = ((bf16[8,16,2048]{2,1,0:T(8,128)(2,1)}), bf16[8,16,2048]{2,1,0:T(8,128)(2,1)S(1)}, u32[]{:S(2)}, u32[]{:S(2)}) async-start(bf16[8,16,2048]{2,1,0:T(8,128)(2,1)} %broadcast_in_dim.24), calls=%async_computation | async-start | bytes 1048576 | tf_op jit(solution)/shard_map/all_to_all | solution.py:286
  39.0 10.6 %collective-permute-start.1 = (bf16[128,8,128]{2,1,0:T(8,128)(2,1)S(1)}, bf16[128,8,128]{2,1,0:T(8,128)(2,1)S(1)}, u32[]{:S(2)}, u32[]{:S(2)}) collective-permute-start(bf16[128,8,128]{2,1,0:T(8,128)(2,1)S(1)} %all_to_all.25.own), channel_id=1, source_target_pairs={{0,1},{1,2},{2,3},{3,0},{4,5},{5,6},{6,7},{7,4},{8,9},{9,10},{10,1... | collective-permute-start | bytes 786440 | tf_op jit(solution)/shard_map/ppermute | solution.py:282
  42.2 14.1 %collective-permute-start.2 = (bf16[128,8,128]{2,1,0:T(8,128)(2,1)S(1)}, bf16[128,8,128]{2,1,0:T(8,128)(2,1)S(1)}, u32[]{:S(2)}, u32[]{:S(2)}) collective-permute-start(bf16[128,8,128]{2,1,0:T(8,128)(2,1)S(1)} %all_to_all.25.own), channel_id=1, source_target_pairs={{0,2},{1,3},{2,0},{3,1},{4,6},{5,7},{6,4},{7,5},{8,10},{9,11},{10,... | collective-permute-start | bytes 786440 | tf_op jit(solution)/shard_map/ppermute | solution.py:282
  46.5 10.9 %collective-permute-start.3 = (bf16[128,8,128]{2,1,0:T(8,128)(2,1)S(1)}, bf16[128,8,128]{2,1,0:T(8,128)(2,1)S(1)}, u32[]{:S(2)}, u32[]{:S(2)}) collective-permute-start(bf16[128,8,128]{2,1,0:T(8,128)(2,1)S(1)} %all_to_all.25.own), channel_id=1, source_target_pairs={{0,3},{1,0},{2,1},{3,2},{4,7},{5,4},{6,5},{7,6},{8,11},{9,8},{10,9... | collective-permute-start | bytes 786440 | tf_op jit(solution)/shard_map/ppermute | solution.py:282
  59.2 8.9 %collective-permute-start.4 = (bf16[128,16,128]{2,1,0:T(8,128)(2,1)S(1)}, bf16[128,16,128]{2,1,0:T(8,128)(2,1)S(1)}, u32[]{:S(2)}, u32[]{:S(2)}) collective-permute-start(bf16[128,16,128]{2,1,0:T(8,128)(2,1)S(1)} %get-tuple-element.8.own), channel_id=1, source_target_pairs={{0,4},{4,0},{1,5},{5,1},{2,6},{6,2},{3,7},{7,3},{8,12},{12,8},{9,1... | collective-permute-start | bytes 1572872 | tf_op jit(solution)/shard_map/ppermute | solution.py:300
  62.6 3.9 %collective-permute-start = (bf16[8,16,2048]{2,1,0:T(8,128)(2,1)S(1)}, bf16[8,16,2048]{2,1,0:T(8,128)(2,1)}, u32[]{:S(2)}, u32[]{:S(2)}) collective-permute-start(bf16[8,16,2048]{2,1,0:T(8,128)(2,1)S(1)} %all-to-all-done.own), channel_id=1, source_target_pairs={{0,4},{4,0},{1,5},{5,1},{2,6},{6,2},{3,7},{7,3},{8,12},{12,8},{9,1... | collective-permute-start | bytes 1572872 | tf_op jit(solution)/shard_map/ppermute | solution.py:288
  66.6 1.6 %copy-start.1 = (bf16[512,768]{1,0:T(8,128)(2,1)S(1)}, bf16[512,768]{1,0:T(8,128)(2,1)}, u32[]{:S(2)}) copy-start(bf16[512,768]{1,0:T(8,128)(2,1)} %constant.77.clone.table) | copy-start | bytes 2359300
  66.6 1.6 %copy-start.3 = (f32[256,16]{1,0:T(8,128)S(1)}, f32[256,16]{1,0:T(8,128)}, u32[]{:S(2)}) copy-start(f32[256,16]{1,0:T(8,128)} %constant.78.clone.twiddles) | copy-start | bytes 49156
  72.7 10.7 %copy-start.6 = (s32[1,1,4,32,1]{3,4,2,1,0:T(1,128)S(1)}, s32[1,1,4,32,1]{3,4,2,1,0:T(1,128)}, u32[]{:S(2)}) copy-start(s32[1,1,4,32,1]{3,4,2,1,0:T(1,128)} %param.17) | copy-start | bytes 1540
  72.7 40.4 %all-to-all-start.2 = ((bf16[128,32,128]{2,1,0:T(8,128)(2,1)}), bf16[128,32,128]{2,1,0:T(8,128)(2,1)S(1)}, u32[]{:S(2)}, u32[]{:S(2)}) async-start(bf16[128,32,128]{2,1,0:T(8,128)(2,1)} %whiten.1), calls=%async_computation.2 | async-start | bytes 2097152 | tf_op jit(solution)/shard_map/all_to_all | solution.py:342
  82.2 0.7 copy-start.7
  84.4 28.8 %copy-start.2 = (bf16[768,256]{1,0:T(8,128)(2,1)S(1)}, bf16[768,256]{1,0:T(8,128)(2,1)}, u32[]{:S(2)}) copy-start(bf16[768,256]{1,0:T(8,128)(2,1)} %constant.80.clone.table) | copy-start | bytes 1179652
  84.9 28.2 %copy-start.4 = (f32[2,16,1,128]{3,2,1,0:T(1,128)S(1)}, f32[2,16,1,128]{3,2,1,0:T(1,128)}, u32[]{:S(2)}) copy-start(f32[2,16,1,128]{3,2,1,0:T(1,128)} %constant.79.clone.turns) | copy-start | bytes 49156
  114.4 8.5 %all-to-all-start.3 = ((bf16[4,32,256]{2,1,0:T(8,128)(2,1)}), bf16[4,32,256]{2,1,0:T(8,128)(2,1)S(1)}, u32[]{:S(2)}, u32[]{:S(2)}) async-start(bf16[4,32,256]{2,1,0:T(8,128)(2,1)} %broadcast_in_dim.46), calls=%async_computation.3 | async-start | bytes 131072 | tf_op jit(solution)/shard_map/all_to_all | solution.py:355

commit v5 on v4

--- a/solution.py
+++ b/solution.py
@@ -19,6 +19,7 @@
 TILE_ROWS = DM // NZ
 RADIX = 8
 INNER = DM // RADIX
+PITCH = RADIX + 1
 ROOT_HALF = math.sqrt(0.5)
 
 f32 = jnp.float32
@@ -198,9 +199,11 @@
     half = TILE_ROWS // NC
     starts = [pl.multiple_of(half * side, half) for side in (place[1], 1 - place[1])]
     halves = [tile[pl.ds(start, half), :] for start in starts]
-    white[...] = dot(left, jnp.concatenate(halves, axis=0)) * row_flip[...]
+    result = dot(left, jnp.concatenate(halves, axis=0)) * row_flip[...]
+    for q in range(INNER):
+        white[PITCH * q : PITCH * q + RADIX, :] = result[RADIX * q : RADIX * (q + 1)]
     for p in range(0, RADIX, 2):
-        pair = [white[pl.ds(p + k, INNER, stride=RADIX), :] for k in range(2)]
+        pair = [white[pl.ds(p + k, INNER, stride=PITCH), :] for k in range(2)]
         part = jnp.concatenate(pair, axis=1)
         part_high, part_low = split_values(part)
         both = dot(table[...], jnp.concatenate([part_high, part_high, part_low], axis=0))
@@ -314,7 +317,7 @@
     local_ids = listed[0, 0, 0] - row_id * (GROUP_ROWS * NYC)
     wanted = (local_ids % NYC) * GROUP_ROWS + local_ids // NYC
     wanted = wanted[:, None]
-    owner_ids = owners[0, 0, :, :, 0].reshape(-1)
+    owner_ids = (owners + e_id // NE)[0, 0, :, :, 0].reshape(-1)
     order = jnp.arange(NE * list_len, dtype=jnp.int32)
     same = (owner_ids[:, None] == owner_ids[None, :]) & (order[:, None] < order[None, :])
     position = owner_ids * capacity + jnp.sum(same.astype(jnp.int32), axis=0)
@@ -333,7 +336,7 @@
         in_specs=[IN_SMEM] + [IN_VMEM] * 6,
         out_specs=IN_VMEM,
         scratch_shapes=[
-            pltpu.VMEM((DM, BLOCK), f32),
+            pltpu.VMEM((PITCH * INNER, BLOCK), f32),
             pltpu.VMEM((RADIX, 2 * INNER, BLOCK), f32),
         ],
         compiler_params=grant(16),

time: 145 us -> 145 us (level)
  no operation moved by 1% of the time
where the time goes in v5:
time: 145 us; the launch traced here: 144 us
  blocking collectives  53.9 us (37%)
  waiting for transfers between devices  41.5 us (29%)
  starting transfers between devices  32.8 us (23%)
  Pallas kernels  9.43 us (7%)
  local copies, waits for them, and re-layouts  3.57 us (2%)
  other arithmetic  2.49 us (2%)
    all_to_all x1, blocking collectives, shards(): pieces = lax.all_to_all(pieces, ROW_AXES, 0, 0, tiled=True)  33.6 us
    all_to_all x1, waiting for transfers between devices, shards(): partial_rows = lax.all_to_all(partial_cols, ROW_AXES, 0, 0, tiled=True)  28.7 us
    all_to_all x1, blocking collectives, shards(): arrived = lax.all_to_all(outgoing, ROW_AXES, 0, 0, tiled=True)  20.4 us
    ppermute x3, starting transfers between devices, shards(): lax.ppermute(pieces, 'e', [(i, (i + step) % NE) for i in range(NE)])  10.5 us
    all_to_all x1, starting transfers between devices, shards(): partial_rows = lax.all_to_all(partial_cols, ROW_AXES, 0, 0, tiled=True)  9.32 us
    ppermute x3, waiting for transfers between devices, shards(): lax.ppermute(pieces, 'e', [(i, (i + step) % NE) for i in range(NE)])  7.78 us
    pallas_call x1, Pallas kernels, shards(): pl.pallas_call(whiten_kernel, out_shape=pltpu.VMEM((ROWS, 2 * GROUP_ROWS,...  4.56 us
    all_to_all x1, waiting for transfers between devices, shards(): lax.all_to_all(jnp.broadcast_to(picked[None], (NE,) + picked.shape), 'e',...  4.47 us
  transfers between devices with their start and end apart: 8, of which 5 were waited for; matrix products, arithmetic and copies ran while one was open for 2% of the time, Pallas kernels for 2%

profile of v5, /device:TPU:1, one launch (start us, length us, event | category | flops | bytes accessed | tf_op | source)
XLA Modules:
  0.0 144.1 jit_solution(15813004491304289436)
XLA Ops:
  0.0 0.0 copy-start
  0.0 1.1 deal.1
  1.1 0.0 copy-start.5
  1.1 33.6 %all_to_all.25.own = bf16[128,8,128]{2,1,0:T(8,128)(2,1)S(1)} all-to-all(bf16[128,8,128]{2,1,0:T(8,128)(2,1)S(1)} %deal.1), channel_id=1, replica_groups=mesh['z'=8,'y'=8,'c'=2,'e'=4] {'z','y','c'}, dimensions={0} | all-to-all | bytes 524288 | tf_op jit(solution)/shard_map/all_to_all | solution.py:283
  34.7 0.0 copy-done.5
  34.7 0.8 broadcast_in_dim.24
  35.5 3.5 %all-to-all-start = ((bf16[8,16,2048]{2,1,0:T(8,128)(2,1)}), bf16[8,16,2048]{2,1,0:T(8,128)(2,1)S(1)}, u32[]{:S(2)}, u32[]{:S(2)}) async-start(bf16[8,16,2048]{2,1,0:T(8,128)(2,1)} %broadcast_in_dim.24), calls=%async_computation | async-start | bytes 1048576 | tf_op jit(solution)/shard_map/all_to_all | solution.py:289
  39.0 3.1 %collective-permute-start.1 = (bf16[128,8,128]{2,1,0:T(8,128)(2,1)S(1)}, bf16[128,8,128]{2,1,0:T(8,128)(2,1)S(1)}, u32[]{:S(2)}, u32[]{:S(2)}) collective-permute-start(bf16[128,8,128]{2,1,0:T(8,128)(2,1)S(1)} %all_to_all.25.own), channel_id=1, source_target_pairs={{0,1},{1,2},{2,3},{3,0},{4,5},{5,6},{6,7},{7,4},{8,9},{9,10},{10,1... | collective-permute-start | bytes 786440 | tf_op jit(solution)/shard_map/ppermute | solution.py:285
  42.2 4.4 %collective-permute-start.2 = (bf16[128,8,128]{2,1,0:T(8,128)(2,1)S(1)}, bf16[128,8,128]{2,1,0:T(8,128)(2,1)S(1)}, u32[]{:S(2)}, u32[]{:S(2)}) collective-permute-start(bf16[128,8,128]{2,1,0:T(8,128)(2,1)S(1)} %all_to_all.25.own), channel_id=1, source_target_pairs={{0,2},{1,3},{2,0},{3,1},{4,6},{5,7},{6,4},{7,5},{8,10},{9,11},{10,... | collective-permute-start | bytes 786440 | tf_op jit(solution)/shard_map/ppermute | solution.py:285
  46.5 3.1 %collective-permute-start.3 = (bf16[128,8,128]{2,1,0:T(8,128)(2,1)S(1)}, bf16[128,8,128]{2,1,0:T(8,128)(2,1)S(1)}, u32[]{:S(2)}, u32[]{:S(2)}) collective-permute-start(bf16[128,8,128]{2,1,0:T(8,128)(2,1)S(1)} %all_to_all.25.own), channel_id=1, source_target_pairs={{0,3},{1,0},{2,1},{3,2},{4,7},{5,4},{6,5},{7,6},{8,11},{9,8},{10,9... | collective-permute-start | bytes 786440 | tf_op jit(solution)/shard_map/ppermute | solution.py:285
  49.6 0.1 pad_add_fusion.place
  49.7 0.0 collective-permute-done.1.first_shared
  49.7 6.5 %collective-permute-done.2.second_shared = bf16[128,8,128]{2,1,0:T(8,128)(2,1)S(1)} collective-permute-done((bf16[128,8,128]{2,1,0:T(8,128)(2,1)S(1)}, bf16[128,8,128]{2,1,0:T(8,128)(2,1)S(1)}, u32[]{:S(2)}, u32[]{:S(2)}) %collective-permute-start.2) | collective-permute-done | bytes 262176 | tf_op jit(solution)/shard_map/ppermute | solution.py:285
  56.2 1.2 collective-permute-done.3.third_shared
  57.5 1.7 %arrange.1 = (bf16[128,16,128]{2,1,0:T(8,128)(2,1)S(1)}, bf16[128,16,128]{2,1,0:T(8,128)(2,1)S(1)}) custom-call(s32[2]{0:T(128)S(1)} %pad_add_fusion.place, bf16[128,8,128]{2,1,0:T(8,128)(2,1)S(1)} %all_to_all.25.own, bf16[128,8,128]{2,1,0:T(8,128)(2,1)S(1)} %collective-permute-done.1.first_shared, ...), custom_call_target="tpu_custom_call" | custom-call | tf_op jit(solution)/shard_map/arrange/pallas_call | solution.py:294
  59.2 3.4 %collective-permute-start.4 = (bf16[128,16,128]{2,1,0:T(8,128)(2,1)S(1)}, bf16[128,16,128]{2,1,0:T(8,128)(2,1)S(1)}, u32[]{:S(2)}, u32[]{:S(2)}) collective-permute-start(bf16[128,16,128]{2,1,0:T(8,128)(2,1)S(1)} %get-tuple-element.8.own), channel_id=1, source_target_pairs={{0,4},{4,0},{1,5},{5,1},{2,6},{6,2},{3,7},{7,3},{8,12},{12,8},{9,1... | collective-permute-start | bytes 1572872 | tf_op jit(solution)/shard_map/ppermute | solution.py:303
  62.6 0.0 all-to-all-done.own
  62.6 1.9 %collective-permute-start = (bf16[8,16,2048]{2,1,0:T(8,128)(2,1)S(1)}, bf16[8,16,2048]{2,1,0:T(8,128)(2,1)}, u32[]{:S(2)}, u32[]{:S(2)}) collective-permute-start(bf16[8,16,2048]{2,1,0:T(8,128)(2,1)S(1)} %all-to-all-done.own), channel_id=1, source_target_pairs={{0,4},{4,0},{1,5},{5,1},{2,6},{6,2},{3,7},{7,3},{8,12},{12,8},{9,1... | collective-permute-start | bytes 1572872 | tf_op jit(solution)/shard_map/ppermute | solution.py:291
  64.5 0.8 convert_bitcast_fusion
  65.3 0.0 copy-done
  65.4 0.1 reshape.203
  65.5 0.4 copy.21.row_flip
  65.9 0.1 select_reduce_fusion
  66.0 0.6 collective-permute-done.other
  66.6 0.0 copy-start.1
  66.6 0.0 copy-start.3
  66.6 1.6 %project.1.tile = bf16[256,128]{1,0:T(8,128)(2,1)S(1)} custom-call(s32[2]{0:T(128)S(1)} %pad_add_fusion.place, bf16[8,16,2048]{2,1,0:T(8,128)(2,1)S(1)} %all-to-all-done.own, bf16[8,16,2048]{2,1,0:T(8,128)(2,1)} %collective-permute-done.other, bf16[128,16,128]{2,1,0:T(8,128)(2,1)S(1)} %get-tuple-element.7.right, f32[1,128]{1,0:T(1,128)S(1)} %convert_bitcast_fusion.1.col_flip), custom_call_target="tpu_custom_call" | custom-call | tf_op jit(solution)/shard_map/project/pallas_call | solution.py:325
  68.1 0.0 collective-permute-done.4.other
  68.1 0.0 copy-done.1
  68.1 0.0 copy-done.3
  68.1 4.6 %whiten.1 = bf16[128,32,128]{2,1,0:T(8,128)(2,1)} custom-call(s32[2]{0:T(128)S(1)} %pad_add_fusion.place, bf16[256,128]{1,0:T(8,128)(2,1)S(1)} %project.1.tile, bf16[128,16,128]{2,1,0:T(8,128)(2,1)S(1)} %get-tuple-element.8.own, bf16[128,16,128]{2,1,0:T(8,128)(2,1)S(1)} %collective-permute-done.4.other, f32[2048,1]{1,0:T(8,128)S(1)} %copy.21.row_flip, ...), custom_call_target="tpu_custom_call" | custom-call | tf_op jit(solution)/shard_map/whiten/pallas_call | solution.py:333
  72.7 9.3 %all-to-all-start.2 = ((bf16[128,32,128]{2,1,0:T(8,128)(2,1)}), bf16[128,32,128]{2,1,0:T(8,128)(2,1)S(1)}, u32[]{:S(2)}, u32[]{:S(2)}) async-start(bf16[128,32,128]{2,1,0:T(8,128)(2,1)} %whiten.1), calls=%async_computation.2 | async-start | bytes 2097152 | tf_op jit(solution)/shard_map/all_to_all | solution.py:345
  82.0 0.0 copy-start.7
  82.1 0.6 copy-done.7
  82.7 0.1 copy.22
  82.8 0.0 copy-start.6
  82.8 0.7 copy-done.6
  83.5 0.1 reshape_squeeze.3
  83.6 0.1 convert_reduce_fusion
  83.7 0.0 copy-start.2
  83.7 0.5 fusion
  84.3 0.0 copy-start.4
  84.3 28.7 %all-to-all-done.2.parts = bf16[128,32,128]{2,1,0:T(8,128)(2,1)S(1)} async-done(((bf16[128,32,128]{2,1,0:T(8,128)(2,1)}), bf16[128,32,128]{2,1,0:T(8,128)(2,1)S(1)}, u32[]{:S(2)}, u32[]{:S(2)}) %all-to-all-start.2) | async-done | bytes 1048608 | tf_op jit(solution)/shard_map/all_to_all | solution.py:345
  113.0 0.0 copy-done.2
  113.0 0.0 copy-done.4
  113.0 0.5 spectrum.1
  113.5 0.6 broadcast_in_dim.46
  114.2 4.1 %all-to-all-start.3 = ((bf16[4,32,256]{2,1,0:T(8,128)(2,1)}), bf16[4,32,256]{2,1,0:T(8,128)(2,1)S(1)}, u32[]{:S(2)}, u32[]{:S(2)}) async-start(bf16[4,32,256]{2,1,0:T(8,128)(2,1)} %broadcast_in_dim.46), calls=%async_computation.3 | async-start | bytes 131072 | tf_op jit(solution)/shard_map/all_to_all | solution.py:358
  118.2 4.5 %all-to-all-done.3 = bf16[4,32,256]{2,1,0:T(8,128)(2,1)S(1)} async-done(((bf16[4,32,256]{2,1,0:T(8,128)(2,1)}), bf16[4,32,256]{2,1,0:T(8,128)(2,1)S(1)}, u32[]{:S(2)}, u32[]{:S(2)}) %all-to-all-start.3) | async-done | bytes 65568 | tf_op jit(solution)/shard_map/all_to_all | solution.py:358
  122.7 0.2 convolution_convert_fusion
  122.9 0.1 reshape.205
  122.9 20.4 %all_to_all.26 = bf16[128,2,256]{2,1,0:T(2,128)(2,1)S(1)} all-to-all(bf16[128,2,256]{2,1,0:T(2,128)(2,1)S(1)} %reshape.205), channel_id=1, replica_groups=mesh['z'=8,'y'=8,'c'=2,'e'=4] {'z','y','c'}, dimensions={0} | all-to-all | bytes 262144 | tf_op jit(solution)/shard_map/all_to_all | solution.py:364
  143.3 0.8 bitcast_convert_fusion
  (11 shorter events, 0.1 us)
Async XLA Ops:
  0.0 65.3 %copy-start = (s32[1,4,2048]{2,1,0:T(4,128)S(1)}, s32[1,4,2048]{2,1,0:T(4,128)}, u32[]{:S(2)}) copy-start(s32[1,4,2048]{2,1,0:T(4,128)} %param.15) | copy-start | bytes 98308
  1.1 33.6 %copy-start.5 = (bf16[1,1,16,2048]{3,2,1,0:T(8,128)(2,1)S(1)}, bf16[1,1,16,2048]{3,2,1,0:T(8,128)(2,1)}, u32[]{:S(2)}) copy-start(bf16[1,1,16,2048]{3,2,1,0:T(8,128)(2,1)} %param.11) | copy-start | bytes 196612
  35.5 27.1 %all-to-all-start = ((bf16[8,16,2048]{2,1,0:T(8,128)(2,1)}), bf16[8,16,2048]{2,1,0:T(8,128)(2,1)S(1)}, u32[]{:S(2)}, u32[]{:S(2)}) async-start(bf16[8,16,2048]{2,1,0:T(8,128)(2,1)} %broadcast_in_dim.24), calls=%async_computation | async-start | bytes 1048576 | tf_op jit(solution)/shard_map/all_to_all | solution.py:289
  39.0 10.6 %collective-permute-start.1 = (bf16[128,8,128]{2,1,0:T(8,128)(2,1)S(1)}, bf16[128,8,128]{2,1,0:T(8,128)(2,1)S(1)}, u32[]{:S(2)}, u32[]{:S(2)}) collective-permute-start(bf16[128,8,128]{2,1,0:T(8,128)(2,1)S(1)} %all_to_all.25.own), channel_id=1, source_target_pairs={{0,1},{1,2},{2,3},{3,0},{4,5},{5,6},{6,7},{7,4},{8,9},{9,10},{10,1... | collective-permute-start | bytes 786440 | tf_op jit(solution)/shard_map/ppermute | solution.py:285
  42.2 14.1 %collective-permute-start.2 = (bf16[128,8,128]{2,1,0:T(8,128)(2,1)S(1)}, bf16[128,8,128]{2,1,0:T(8,128)(2,1)S(1)}, u32[]{:S(2)}, u32[]{:S(2)}) collective-permute-start(bf16[128,8,128]{2,1,0:T(8,128)(2,1)S(1)} %all_to_all.25.own), channel_id=1, source_target_pairs={{0,2},{1,3},{2,0},{3,1},{4,6},{5,7},{6,4},{7,5},{8,10},{9,11},{10,... | collective-permute-start | bytes 786440 | tf_op jit(solution)/shard_map/ppermute | solution.py:285
  46.5 10.9 %collective-permute-start.3 = (bf16[128,8,128]{2,1,0:T(8,128)(2,1)S(1)}, bf16[128,8,128]{2,1,0:T(8,128)(2,1)S(1)}, u32[]{:S(2)}, u32[]{:S(2)}) collective-permute-start(bf16[128,8,128]{2,1,0:T(8,128)(2,1)S(1)} %all_to_all.25.own), channel_id=1, source_target_pairs={{0,3},{1,0},{2,1},{3,2},{4,7},{5,4},{6,5},{7,6},{8,11},{9,8},{10,9... | collective-permute-start | bytes 786440 | tf_op jit(solution)/shard_map/ppermute | solution.py:285
  59.2 8.9 %collective-permute-start.4 = (bf16[128,16,128]{2,1,0:T(8,128)(2,1)S(1)}, bf16[128,16,128]{2,1,0:T(8,128)(2,1)S(1)}, u32[]{:S(2)}, u32[]{:S(2)}) collective-permute-start(bf16[128,16,128]{2,1,0:T(8,128)(2,1)S(1)} %get-tuple-element.8.own), channel_id=1, source_target_pairs={{0,4},{4,0},{1,5},{5,1},{2,6},{6,2},{3,7},{7,3},{8,12},{12,8},{9,1... | collective-permute-start | bytes 1572872 | tf_op jit(solution)/shard_map/ppermute | solution.py:303
  62.6 3.9 %collective-permute-start = (bf16[8,16,2048]{2,1,0:T(8,128)(2,1)S(1)}, bf16[8,16,2048]{2,1,0:T(8,128)(2,1)}, u32[]{:S(2)}, u32[]{:S(2)}) collective-permute-start(bf16[8,16,2048]{2,1,0:T(8,128)(2,1)S(1)} %all-to-all-done.own), channel_id=1, source_target_pairs={{0,4},{4,0},{1,5},{5,1},{2,6},{6,2},{3,7},{7,3},{8,12},{12,8},{9,1... | collective-permute-start | bytes 1572872 | tf_op jit(solution)/shard_map/ppermute | solution.py:291
  66.6 1.6 %copy-start.1 = (bf16[512,768]{1,0:T(8,128)(2,1)S(1)}, bf16[512,768]{1,0:T(8,128)(2,1)}, u32[]{:S(2)}) copy-start(bf16[512,768]{1,0:T(8,128)(2,1)} %constant.89.clone.table) | copy-start | bytes 2359300
  66.6 1.6 %copy-start.3 = (f32[256,16]{1,0:T(8,128)S(1)}, f32[256,16]{1,0:T(8,128)}, u32[]{:S(2)}) copy-start(f32[256,16]{1,0:T(8,128)} %constant.90.clone.twiddles) | copy-start | bytes 49156
  72.7 40.3 %all-to-all-start.2 = ((bf16[128,32,128]{2,1,0:T(8,128)(2,1)}), bf16[128,32,128]{2,1,0:T(8,128)(2,1)S(1)}, u32[]{:S(2)}, u32[]{:S(2)}) async-start(bf16[128,32,128]{2,1,0:T(8,128)(2,1)} %whiten.1), calls=%async_computation.2 | async-start | bytes 2097152 | tf_op jit(solution)/shard_map/all_to_all | solution.py:345
  82.0 0.7 copy-start.7
  82.8 0.7 copy-start.6
  83.7 29.3 %copy-start.2 = (bf16[768,256]{1,0:T(8,128)(2,1)S(1)}, bf16[768,256]{1,0:T(8,128)(2,1)}, u32[]{:S(2)}) copy-start(bf16[768,256]{1,0:T(8,128)(2,1)} %constant.92.clone.table) | copy-start | bytes 1179652
  84.3 28.7 %copy-start.4 = (f32[2,16,1,128]{3,2,1,0:T(1,128)S(1)}, f32[2,16,1,128]{3,2,1,0:T(1,128)}, u32[]{:S(2)}) copy-start(f32[2,16,1,128]{3,2,1,0:T(1,128)} %constant.91.clone.turns) | copy-start | bytes 49156
  114.2 8.5 %all-to-all-start.3 = ((bf16[4,32,256]{2,1,0:T(8,128)(2,1)}), bf16[4,32,256]{2,1,0:T(8,128)(2,1)S(1)}, u32[]{:S(2)}, u32[]{:S(2)}) async-start(bf16[4,32,256]{2,1,0:T(8,128)(2,1)} %broadcast_in_dim.46), calls=%async_computation.3 | async-start | bytes 131072 | tf_op jit(solution)/shard_map/all_to_all | solution.py:358
